TPU v7x, 32 devices: a whole 2x2x4 slice. The times are simulated.
32 devices in a mesh: groups: 2 (over x), tm: 16 (over z, y, core).
Axes of the slice: x: 2, y: 2, z: 4, core: 2. Of those that a mesh axis runs over, the one named last changes fastest.
Arguments:
- points: float32 [32, 64, 2048], P(('groups', 'tm')), parts along dimension 0, may hold values from -4 to 4
- potentials: float32 [32, 224, 2048], P(('groups', 'tm')), parts along dimension 0, may hold values from 0.5 to 25, as said below
- supports: int32 [32], P(('groups', 'tm')), parts along dimension 0, may hold values from 512 to 2048, as said below
Outputs:
- messages: float32 [32, 224, 2048], P(('groups', 'tm')), parts along dimension 0
- log_scale: float32 [448], P('groups'), parts along dimension 0
There are 2 independent parts, one for each index of `groups`. A program takes and returns all parts, laid end to end along the dimension named above; each array names one. Nothing has to cross between parts.
Inputs may be any that keep to these rules, and one draw needn't show every extreme that they name: `supports`: the first and the last time slice have all 2048 points live; every other slice has between 512 and 1024 live points, at its first positions. `potentials`: positive scalings.
All inputs are finite; a program needn't handle non-finite values.
Results may differ from a plain program's by a relative error of at most 0.017.
Values may be sent and summed in bfloat16 or wider, within the bound.
No kernel may reach another device: no remote copies, remote signals or barrier semaphores. Data moves between devices by JAX's collectives and lax.ppermute only.
A program may use at most 64 MiB of HBM per device.

v0:
```python
import jax
import jax.numpy as jnp
from jax import lax
from jax.sharding import PartitionSpec as P

MICRO = 32


A_DECAY = 0.8
EPS_SCALE = 0.05


def shifted(value, axis, steps):
    count = lax.axis_size(axis)
    initial, last = (max(0, -steps), min(count, count - steps))
    return lax.ppermute(value, axis, [(source, source + steps) for source in range(initial, last)])


def slice_kernel(source, target):
    dim_count, point_count = source.shape
    block_rows = min(512, point_count)
    inv_width = 1.0 / (2.0 * EPS_SCALE * dim_count)
    target_sq = jnp.sum(target * target, axis=0)
    pieces = jnp.transpose(
        source.reshape(dim_count, point_count // block_rows, block_rows), (1, 0, 2)
    )

    def one_block(segment):
        products = lax.dot_general(
            segment,
            target,
            (((0,), (0,)), ((), ())),
            precision=lax.Precision.HIGHEST,
            preferred_element_type=jnp.float32,
        )
        segment_sq = jnp.sum(segment * segment, axis=0)
        distance = (
            target_sq[None, :] + A_DECAY * A_DECAY * segment_sq[:, None] - 2.0 * A_DECAY * products
        )
        return jnp.exp(-inv_width * distance).astype(jnp.bfloat16)

    return lax.map(one_block, pieces).reshape(point_count, point_count)


def push_forward(weighted, kernel, live_row):
    pushed = jnp.dot(weighted, kernel, preferred_element_type=jnp.float32) * live_row[None, :]
    return (pushed, jnp.sum(pushed, axis=1))


def per_device(points, potentials, supports):
    local_slices, dim_count, point_count = points.shape
    all_cols = potentials.shape[1]
    tm_count = lax.axis_size("tm")
    position = lax.axis_index("tm")
    live_mask = (jnp.arange(point_count, dtype=jnp.int32)[None, :] < supports[:, None]).astype(
        jnp.float32
    )
    counts = supports.astype(jnp.float32)
    arrived = shifted(points[local_slices - 1], "tm", 1)
    sources = jnp.concatenate([arrived[None], points[:-1]], axis=0)
    kernels = lax.map(lambda paired: slice_kernel(paired[0], paired[1]), (sources, points))
    block_cols = MICRO
    batches = all_cols // block_cols
    phase_count = tm_count + batches - 1
    is_first = position == 0

    def section(incoming, block_id):
        block_pot = lax.dynamic_slice_in_dim(potentials, block_id * block_cols, block_cols, 1)
        pushed, column_sum = push_forward(incoming, kernels[0], live_mask[0])
        safe_sum = jnp.where(is_first, 1.0, column_sum)
        start_msg = jnp.broadcast_to(live_mask[0][None, :], pushed.shape)
        message = jnp.where(is_first, start_msg, pushed * (counts[0] / safe_sum)[:, None])
        outputs = [message]
        log_terms = [jnp.where(is_first, 0.0, jnp.log(safe_sum / counts[0]))]
        outgoing = (message * block_pot[local_slices - 1]).astype(jnp.bfloat16)
        return (jnp.stack(outputs), jnp.stack(log_terms), outgoing)

    def advance(phase, state_in):
        incoming, messages, log_parts = state_in
        block_id = phase - position
        active = (block_id >= 0) & (block_id < batches)
        clipped = jnp.clip(block_id, 0, batches - 1)

        def compute(operands):
            stored, stored_logs = operands
            block_msgs, block_logs, outgoing = section(incoming, clipped)
            stored = lax.dynamic_update_slice_in_dim(stored, block_msgs, clipped * block_cols, 1)
            stored_logs = lax.dynamic_update_slice_in_dim(
                stored_logs, block_logs, clipped * block_cols, 1
            )
            return (stored, stored_logs, outgoing)

        def skipped(operands):
            stored, stored_logs = operands
            return (stored, stored_logs, jnp.zeros((block_cols, point_count), jnp.bfloat16))

        messages, log_parts, outgoing = lax.cond(active, compute, skipped, (messages, log_parts))
        received = shifted(outgoing, "tm", 1)
        return (received, messages, log_parts)

    initial = (
        jnp.zeros((block_cols, point_count), jnp.bfloat16),
        jnp.zeros((local_slices, all_cols, point_count), jnp.float32),
        jnp.zeros((local_slices, all_cols), jnp.float32),
    )
    unused, messages, log_parts = lax.fori_loop(0, phase_count, advance, initial)
    local_log = jnp.sum(log_parts, axis=0)
    log_scale = lax.psum(local_log, "tm") / (tm_count * local_slices - 1)
    return (messages, log_scale)


def solution(mesh):
    placed = (P(("groups", "tm"), None, None), P(("groups", "tm"), None, None), P(("groups", "tm")))
    return jax.shard_map(
        per_device,
        mesh=mesh,
        in_specs=placed,
        out_specs=(P(("groups", "tm"), None, None), P("groups")),
        check_vma=False,
    )
```

profile of v0, /device:TPU:0, one launch (start us, length us, event | category | flops | bytes accessed | tf_op | source)
XLA Modules:
  0.0 334.8 jit_solution(13703646366627489090)
XLA Ops:
  4.9 26.2 %while.35 = (s32[]{:T(128)}, bf16[4,512,2048]{2,1,0:T(8,128)(2,1)}, f32[2048]{0:T(1024)S(1)}, f32[4,64,512]{2,1,0:T(8,128)S(1)}, f32[64,2048]{1,0:T(8,128)}, /*index=5*/s32[]{:T(128)}) while((s32[]{:T(128)}, bf16[4,512,2048]{2,1,0:T(8,128)(2,1)}, f32[2048]{0:T(1024)S(1)}, f32[4,64,512]{2,1,0:T(8,128)S(1)}, f32[64,2048]{1,0:T(8,128)}, ...), condition=%wide.region_3.0_spmd, body=%wide.region_1.3_spmd.sunk | while | flops 810614784 | bytes 2901065 | solution.py:42
  4.9 6.5 %fusion.26 = bf16[4,512,2048]{2,1,0:T(8,128)(2,1)} fusion(bf16[4,512,2048]{2,1,0:T(8,128)(2,1)} %get-tuple-element.449, s32[]{:T(128)} %get-tuple-element.448, f32[64,2048]{1,0:T(8,128)} %get-tuple-element.458, f32[512]{0:T(512)S(1)} %broadcast_multiply_fusion.3, f32[2048]{0:T(1024)S(1)} %get-tuple-element.456, f32[4,64,512]{2,1,0:T(8,128)S(1)} %get-tuple-element.457), kind=kOutput, calls=%fused_computation.3.clone.1 | convolution fusion | flops 810549248 | bytes 2763776 | tf_op jit(solution)/shard_map/while/body/eval_jaxpr/while/body/eval_jaxpr/dot_general | solution.py:29
  11.5 6.5 %fusion.26 = bf16[4,512,2048]{2,1,0:T(8,128)(2,1)} fusion(bf16[4,512,2048]{2,1,0:T(8,128)(2,1)} %get-tuple-element.449, s32[]{:T(128)} %get-tuple-element.448, f32[64,2048]{1,0:T(8,128)} %get-tuple-element.458, f32[512]{0:T(512)S(1)} %broadcast_multiply_fusion.3, f32[2048]{0:T(1024)S(1)} %get-tuple-element.456, f32[4,64,512]{2,1,0:T(8,128)S(1)} %get-tuple-element.457), kind=kOutput, calls=%fused_computation.3.clone.1 | convolution fusion | flops 810549248 | bytes 2763776 | tf_op jit(solution)/shard_map/while/body/eval_jaxpr/while/body/eval_jaxpr/dot_general | solution.py:29
  18.1 6.5 %fusion.26 = bf16[4,512,2048]{2,1,0:T(8,128)(2,1)} fusion(bf16[4,512,2048]{2,1,0:T(8,128)(2,1)} %get-tuple-element.449, s32[]{:T(128)} %get-tuple-element.448, f32[64,2048]{1,0:T(8,128)} %get-tuple-element.458, f32[512]{0:T(512)S(1)} %broadcast_multiply_fusion.3, f32[2048]{0:T(1024)S(1)} %get-tuple-element.456, f32[4,64,512]{2,1,0:T(8,128)S(1)} %get-tuple-element.457), kind=kOutput, calls=%fused_computation.3.clone.1 | convolution fusion | flops 810549248 | bytes 2763776 | tf_op jit(solution)/shard_map/while/body/eval_jaxpr/while/body/eval_jaxpr/dot_general | solution.py:29
  24.6 6.5 %fusion.26 = bf16[4,512,2048]{2,1,0:T(8,128)(2,1)} fusion(bf16[4,512,2048]{2,1,0:T(8,128)(2,1)} %get-tuple-element.449, s32[]{:T(128)} %get-tuple-element.448, f32[64,2048]{1,0:T(8,128)} %get-tuple-element.458, f32[512]{0:T(512)S(1)} %broadcast_multiply_fusion.3, f32[2048]{0:T(1024)S(1)} %get-tuple-element.456, f32[4,64,512]{2,1,0:T(8,128)S(1)} %get-tuple-element.457), kind=kOutput, calls=%fused_computation.3.clone.1 | convolution fusion | flops 810549248 | bytes 2763776 | tf_op jit(solution)/shard_map/while/body/eval_jaxpr/while/body/eval_jaxpr/dot_general | solution.py:29
  31.4 226.2 %while.36 = (s32[]{:T(128)}, bf16[32,2048]{1,0:T(8,128)(2,1)S(1)}, f32[1,224,2048]{2,1,0:T(8,128)S(1)}, f32[1,224]{1,0:T(1,128)S(1)}, s32[]{:T(128)}, /*index=5*...) while((s32[]{:T(128)}, bf16[32,2048]{1,0:T(8,128)(2,1)S(1)}, ...), condition=%wide.region_8.9_spmd.clone, body=%wide.region_4.8_spmd.clone.sunk | while | flops 268963936 | bytes 10520344 | solution.py:106
  32.0 6.4 %conditional.3 = (f32[1,224,2048]{2,1,0:T(8,128)S(1)}, f32[1,224]{1,0:T(1,128)S(1)}, bf16[32,2048]{1,0:T(8,128)(2,1)S(1)}) conditional(s32[]{:T(128)} %convert_element_type.47, (f32[1,224,2048]{2,1,0:T(8,128)S(1)}, f32[1,224]{1,0:T(1,128)S(1)}) %tuple.68, (pred[]{:T(512)}, f32[1,2048]{1,0:T(1,128)S(1)}, bf16[1,2048,2048]{2,1,0:T(8,128)(2,1)}, ...), branch_computations={%region_5.5_spmd, %region_6.7_spmd} | conditional | flops 268959840 | bytes 9987569 | solution.py:97
  42.9 6.5 %conditional.3 = (f32[1,224,2048]{2,1,0:T(8,128)S(1)}, f32[1,224]{1,0:T(1,128)S(1)}, bf16[32,2048]{1,0:T(8,128)(2,1)S(1)}) conditional(s32[]{:T(128)} %convert_element_type.47, (f32[1,224,2048]{2,1,0:T(8,128)S(1)}, f32[1,224]{1,0:T(1,128)S(1)}) %tuple.68, (pred[]{:T(512)}, f32[1,2048]{1,0:T(1,128)S(1)}, bf16[1,2048,2048]{2,1,0:T(8,128)(2,1)}, ...), branch_computations={%region_5.5_spmd, %region_6.7_spmd} | conditional | flops 268959840 | bytes 9987569 | solution.py:97
  56.2 6.5 %conditional.3 = (f32[1,224,2048]{2,1,0:T(8,128)S(1)}, f32[1,224]{1,0:T(1,128)S(1)}, bf16[32,2048]{1,0:T(8,128)(2,1)S(1)}) conditional(s32[]{:T(128)} %convert_element_type.47, (f32[1,224,2048]{2,1,0:T(8,128)S(1)}, f32[1,224]{1,0:T(1,128)S(1)}) %tuple.68, (pred[]{:T(512)}, f32[1,2048]{1,0:T(1,128)S(1)}, bf16[1,2048,2048]{2,1,0:T(8,128)(2,1)}, ...), branch_computations={%region_5.5_spmd, %region_6.7_spmd} | conditional | flops 268959840 | bytes 9987569 | solution.py:97
  67.2 6.5 %conditional.3 = (f32[1,224,2048]{2,1,0:T(8,128)S(1)}, f32[1,224]{1,0:T(1,128)S(1)}, bf16[32,2048]{1,0:T(8,128)(2,1)S(1)}) conditional(s32[]{:T(128)} %convert_element_type.47, (f32[1,224,2048]{2,1,0:T(8,128)S(1)}, f32[1,224]{1,0:T(1,128)S(1)}) %tuple.68, (pred[]{:T(512)}, f32[1,2048]{1,0:T(1,128)S(1)}, bf16[1,2048,2048]{2,1,0:T(8,128)(2,1)}, ...), branch_computations={%region_5.5_spmd, %region_6.7_spmd} | conditional | flops 268959840 | bytes 9987569 | solution.py:97
  80.6 6.4 %conditional.3 = (f32[1,224,2048]{2,1,0:T(8,128)S(1)}, f32[1,224]{1,0:T(1,128)S(1)}, bf16[32,2048]{1,0:T(8,128)(2,1)S(1)}) conditional(s32[]{:T(128)} %convert_element_type.47, (f32[1,224,2048]{2,1,0:T(8,128)S(1)}, f32[1,224]{1,0:T(1,128)S(1)}) %tuple.68, (pred[]{:T(512)}, f32[1,2048]{1,0:T(1,128)S(1)}, bf16[1,2048,2048]{2,1,0:T(8,128)(2,1)}, ...), branch_computations={%region_5.5_spmd, %region_6.7_spmd} | conditional | flops 268959840 | bytes 9987569 | solution.py:97
  94.1 6.5 %conditional.3 = (f32[1,224,2048]{2,1,0:T(8,128)S(1)}, f32[1,224]{1,0:T(1,128)S(1)}, bf16[32,2048]{1,0:T(8,128)(2,1)S(1)}) conditional(s32[]{:T(128)} %convert_element_type.47, (f32[1,224,2048]{2,1,0:T(8,128)S(1)}, f32[1,224]{1,0:T(1,128)S(1)}) %tuple.68, (pred[]{:T(512)}, f32[1,2048]{1,0:T(1,128)S(1)}, bf16[1,2048,2048]{2,1,0:T(8,128)(2,1)}, ...), branch_computations={%region_5.5_spmd, %region_6.7_spmd} | conditional | flops 268959840 | bytes 9987569 | solution.py:97
  107.5 6.5 %conditional.3 = (f32[1,224,2048]{2,1,0:T(8,128)S(1)}, f32[1,224]{1,0:T(1,128)S(1)}, bf16[32,2048]{1,0:T(8,128)(2,1)S(1)}) conditional(s32[]{:T(128)} %convert_element_type.47, (f32[1,224,2048]{2,1,0:T(8,128)S(1)}, f32[1,224]{1,0:T(1,128)S(1)}) %tuple.68, (pred[]{:T(512)}, f32[1,2048]{1,0:T(1,128)S(1)}, bf16[1,2048,2048]{2,1,0:T(8,128)(2,1)}, ...), branch_computations={%region_5.5_spmd, %region_6.7_spmd} | conditional | flops 268959840 | bytes 9987569 | solution.py:97
  121.1 11.7 %collective-permute-start = (bf16[32,2048]{1,0:T(8,128)(2,1)S(1)}, bf16[32,2048]{1,0:T(8,128)(2,1)S(1)}, u32[]{:S(2)}, u32[]{:S(2)}) collective-permute-start(bf16[32,2048]{1,0:T(8,128)(2,1)S(1)} %get-tuple-element.433), channel_id=1, source_target_pairs={{0,1},{1,2},{2,3},{3,4},{4,5},{5,6},{6,7},{7,8},{8,9},{9,10},{10,1... | collective-permute-start | bytes 393224 | tf_op jit(solution)/shard_map/while/body/eval_jaxpr/ppermute | solution.py:16
  141.5 11.8 %collective-permute-start = (bf16[32,2048]{1,0:T(8,128)(2,1)S(1)}, bf16[32,2048]{1,0:T(8,128)(2,1)S(1)}, u32[]{:S(2)}, u32[]{:S(2)}) collective-permute-start(bf16[32,2048]{1,0:T(8,128)(2,1)S(1)} %get-tuple-element.433), channel_id=1, source_target_pairs={{0,1},{1,2},{2,3},{3,4},{4,5},{5,6},{6,7},{7,8},{8,9},{9,10},{10,1... | collective-permute-start | bytes 393224 | tf_op jit(solution)/shard_map/while/body/eval_jaxpr/ppermute | solution.py:16
  162.0 7.3 %collective-permute-start = (bf16[32,2048]{1,0:T(8,128)(2,1)S(1)}, bf16[32,2048]{1,0:T(8,128)(2,1)S(1)}, u32[]{:S(2)}, u32[]{:S(2)}) collective-permute-start(bf16[32,2048]{1,0:T(8,128)(2,1)S(1)} %get-tuple-element.433), channel_id=1, source_target_pairs={{0,1},{1,2},{2,3},{3,4},{4,5},{5,6},{6,7},{7,8},{8,9},{9,10},{10,1... | collective-permute-start | bytes 393224 | tf_op jit(solution)/shard_map/while/body/eval_jaxpr/ppermute | solution.py:16
  170.9 6.2 %collective-permute-start = (bf16[32,2048]{1,0:T(8,128)(2,1)S(1)}, bf16[32,2048]{1,0:T(8,128)(2,1)S(1)}, u32[]{:S(2)}, u32[]{:S(2)}) collective-permute-start(bf16[32,2048]{1,0:T(8,128)(2,1)S(1)} %get-tuple-element.433), channel_id=1, source_target_pairs={{0,1},{1,2},{2,3},{3,4},{4,5},{5,6},{6,7},{7,8},{8,9},{9,10},{10,1... | collective-permute-start | bytes 393224 | tf_op jit(solution)/shard_map/while/body/eval_jaxpr/ppermute | solution.py:16
  178.8 12.7 %collective-permute-start = (bf16[32,2048]{1,0:T(8,128)(2,1)S(1)}, bf16[32,2048]{1,0:T(8,128)(2,1)S(1)}, u32[]{:S(2)}, u32[]{:S(2)}) collective-permute-start(bf16[32,2048]{1,0:T(8,128)(2,1)S(1)} %get-tuple-element.433), channel_id=1, source_target_pairs={{0,1},{1,2},{2,3},{3,4},{4,5},{5,6},{6,7},{7,8},{8,9},{9,10},{10,1... | collective-permute-start | bytes 393224 | tf_op jit(solution)/shard_map/while/body/eval_jaxpr/ppermute | solution.py:16
  193.2 6.2 %collective-permute-start = (bf16[32,2048]{1,0:T(8,128)(2,1)S(1)}, bf16[32,2048]{1,0:T(8,128)(2,1)S(1)}, u32[]{:S(2)}, u32[]{:S(2)}) collective-permute-start(bf16[32,2048]{1,0:T(8,128)(2,1)S(1)} %get-tuple-element.433), channel_id=1, source_target_pairs={{0,1},{1,2},{2,3},{3,4},{4,5},{5,6},{6,7},{7,8},{8,9},{9,10},{10,1... | collective-permute-start | bytes 393224 | tf_op jit(solution)/shard_map/while/body/eval_jaxpr/ppermute | solution.py:16
  201.1 6.2 %collective-permute-start = (bf16[32,2048]{1,0:T(8,128)(2,1)S(1)}, bf16[32,2048]{1,0:T(8,128)(2,1)S(1)}, u32[]{:S(2)}, u32[]{:S(2)}) collective-permute-start(bf16[32,2048]{1,0:T(8,128)(2,1)S(1)} %get-tuple-element.433), channel_id=1, source_target_pairs={{0,1},{1,2},{2,3},{3,4},{4,5},{5,6},{6,7},{7,8},{8,9},{9,10},{10,1... | collective-permute-start | bytes 393224 | tf_op jit(solution)/shard_map/while/body/eval_jaxpr/ppermute | solution.py:16
  216.9 6.7 %collective-permute-start = (bf16[32,2048]{1,0:T(8,128)(2,1)S(1)}, bf16[32,2048]{1,0:T(8,128)(2,1)S(1)}, u32[]{:S(2)}, u32[]{:S(2)}) collective-permute-start(bf16[32,2048]{1,0:T(8,128)(2,1)S(1)} %get-tuple-element.433), channel_id=1, source_target_pairs={{0,1},{1,2},{2,3},{3,4},{4,5},{5,6},{6,7},{7,8},{8,9},{9,10},{10,1... | collective-permute-start | bytes 393224 | tf_op jit(solution)/shard_map/while/body/eval_jaxpr/ppermute | solution.py:16
  225.2 6.2 %collective-permute-start = (bf16[32,2048]{1,0:T(8,128)(2,1)S(1)}, bf16[32,2048]{1,0:T(8,128)(2,1)S(1)}, u32[]{:S(2)}, u32[]{:S(2)}) collective-permute-start(bf16[32,2048]{1,0:T(8,128)(2,1)S(1)} %get-tuple-element.433), channel_id=1, source_target_pairs={{0,1},{1,2},{2,3},{3,4},{4,5},{5,6},{6,7},{7,8},{8,9},{9,10},{10,1... | collective-permute-start | bytes 393224 | tf_op jit(solution)/shard_map/while/body/eval_jaxpr/ppermute | solution.py:16
  249.0 7.6 %collective-permute-start = (bf16[32,2048]{1,0:T(8,128)(2,1)S(1)}, bf16[32,2048]{1,0:T(8,128)(2,1)S(1)}, u32[]{:S(2)}, u32[]{:S(2)}) collective-permute-start(bf16[32,2048]{1,0:T(8,128)(2,1)S(1)} %get-tuple-element.433), channel_id=1, source_target_pairs={{0,1},{1,2},{2,3},{3,4},{4,5},{5,6},{6,7},{7,8},{8,9},{9,10},{10,1... | collective-permute-start | bytes 393224 | tf_op jit(solution)/shard_map/while/body/eval_jaxpr/ppermute | solution.py:16
  257.6 76.6 %psum.7 = f32[224]{0:T(256)S(1)} all-reduce(f32[224]{0:T(256)S(1)} %bitcast.57), channel_id=1, replica_groups=mesh['groups'=2,'tm'=16] {'tm'}, use_global_device_ids=true, to_apply=%region_9.10 | all-reduce | flops 224 | bytes 1792 | tf_op jit(solution)/shard_map/psum | solution.py:108
  (140 shorter events, 147.1 us)
Async XLA Ops:
  0.6 4.2 %collective-permute-start.1 = (f32[64,2048]{1,0:T(8,128)}, f32[64,2048]{1,0:T(8,128)S(1)}, u32[]{:S(2)}, u32[]{:S(2)}) collective-permute-start(f32[64,2048]{1,0:T(8,128)} %bitcast.54), channel_id=1, source_target_pairs={{0,1},{1,2},{2,3},{3,4},{4,5},{5,6},{6,7},{7,8},{8,9},{9,10},{10,1... | collective-permute-start | bytes 1572872 | tf_op jit(solution)/shard_map/ppermute | solution.py:16
  38.5 3.7 %collective-permute-start = (bf16[32,2048]{1,0:T(8,128)(2,1)S(1)}, bf16[32,2048]{1,0:T(8,128)(2,1)S(1)}, u32[]{:S(2)}, u32[]{:S(2)}) collective-permute-start(bf16[32,2048]{1,0:T(8,128)(2,1)S(1)} %get-tuple-element.433), channel_id=1, source_target_pairs={{0,1},{1,2},{2,3},{3,4},{4,5},{5,6},{6,7},{7,8},{8,9},{9,10},{10,1... | collective-permute-start | bytes 393224 | tf_op jit(solution)/shard_map/while/body/eval_jaxpr/ppermute | solution.py:16
  49.4 6.1 %collective-permute-start = (bf16[32,2048]{1,0:T(8,128)(2,1)S(1)}, bf16[32,2048]{1,0:T(8,128)(2,1)S(1)}, u32[]{:S(2)}, u32[]{:S(2)}) collective-permute-start(bf16[32,2048]{1,0:T(8,128)(2,1)S(1)} %get-tuple-element.433), channel_id=1, source_target_pairs={{0,1},{1,2},{2,3},{3,4},{4,5},{5,6},{6,7},{7,8},{8,9},{9,10},{10,1... | collective-permute-start | bytes 393224 | tf_op jit(solution)/shard_map/while/body/eval_jaxpr/ppermute | solution.py:16
  62.7 3.9 %collective-permute-start = (bf16[32,2048]{1,0:T(8,128)(2,1)S(1)}, bf16[32,2048]{1,0:T(8,128)(2,1)S(1)}, u32[]{:S(2)}, u32[]{:S(2)}) collective-permute-start(bf16[32,2048]{1,0:T(8,128)(2,1)S(1)} %get-tuple-element.433), channel_id=1, source_target_pairs={{0,1},{1,2},{2,3},{3,4},{4,5},{5,6},{6,7},{7,8},{8,9},{9,10},{10,1... | collective-permute-start | bytes 393224 | tf_op jit(solution)/shard_map/while/body/eval_jaxpr/ppermute | solution.py:16
  73.8 6.2 %collective-permute-start = (bf16[32,2048]{1,0:T(8,128)(2,1)S(1)}, bf16[32,2048]{1,0:T(8,128)(2,1)S(1)}, u32[]{:S(2)}, u32[]{:S(2)}) collective-permute-start(bf16[32,2048]{1,0:T(8,128)(2,1)S(1)} %get-tuple-element.433), channel_id=1, source_target_pairs={{0,1},{1,2},{2,3},{3,4},{4,5},{5,6},{6,7},{7,8},{8,9},{9,10},{10,1... | collective-permute-start | bytes 393224 | tf_op jit(solution)/shard_map/while/body/eval_jaxpr/ppermute | solution.py:16
  87.1 6.4 %collective-permute-start = (bf16[32,2048]{1,0:T(8,128)(2,1)S(1)}, bf16[32,2048]{1,0:T(8,128)(2,1)S(1)}, u32[]{:S(2)}, u32[]{:S(2)}) collective-permute-start(bf16[32,2048]{1,0:T(8,128)(2,1)S(1)} %get-tuple-element.433), channel_id=1, source_target_pairs={{0,1},{1,2},{2,3},{3,4},{4,5},{5,6},{6,7},{7,8},{8,9},{9,10},{10,1... | collective-permute-start | bytes 393224 | tf_op jit(solution)/shard_map/while/body/eval_jaxpr/ppermute | solution.py:16
  100.6 6.2 %collective-permute-start = (bf16[32,2048]{1,0:T(8,128)(2,1)S(1)}, bf16[32,2048]{1,0:T(8,128)(2,1)S(1)}, u32[]{:S(2)}, u32[]{:S(2)}) collective-permute-start(bf16[32,2048]{1,0:T(8,128)(2,1)S(1)} %get-tuple-element.433), channel_id=1, source_target_pairs={{0,1},{1,2},{2,3},{3,4},{4,5},{5,6},{6,7},{7,8},{8,9},{9,10},{10,1... | collective-permute-start | bytes 393224 | tf_op jit(solution)/shard_map/while/body/eval_jaxpr/ppermute | solution.py:16
  114.0 6.4 %collective-permute-start = (bf16[32,2048]{1,0:T(8,128)(2,1)S(1)}, bf16[32,2048]{1,0:T(8,128)(2,1)S(1)}, u32[]{:S(2)}, u32[]{:S(2)}) collective-permute-start(bf16[32,2048]{1,0:T(8,128)(2,1)S(1)} %get-tuple-element.433), channel_id=1, source_target_pairs={{0,1},{1,2},{2,3},{3,4},{4,5},{5,6},{6,7},{7,8},{8,9},{9,10},{10,1... | collective-permute-start | bytes 393224 | tf_op jit(solution)/shard_map/while/body/eval_jaxpr/ppermute | solution.py:16
  121.1 12.7 %collective-permute-start = (bf16[32,2048]{1,0:T(8,128)(2,1)S(1)}, bf16[32,2048]{1,0:T(8,128)(2,1)S(1)}, u32[]{:S(2)}, u32[]{:S(2)}) collective-permute-start(bf16[32,2048]{1,0:T(8,128)(2,1)S(1)} %get-tuple-element.433), channel_id=1, source_target_pairs={{0,1},{1,2},{2,3},{3,4},{4,5},{5,6},{6,7},{7,8},{8,9},{9,10},{10,1... | collective-permute-start | bytes 393224 | tf_op jit(solution)/shard_map/while/body/eval_jaxpr/ppermute | solution.py:16
  134.5 6.3 %collective-permute-start = (bf16[32,2048]{1,0:T(8,128)(2,1)S(1)}, bf16[32,2048]{1,0:T(8,128)(2,1)S(1)}, u32[]{:S(2)}, u32[]{:S(2)}) collective-permute-start(bf16[32,2048]{1,0:T(8,128)(2,1)S(1)} %get-tuple-element.433), channel_id=1, source_target_pairs={{0,1},{1,2},{2,3},{3,4},{4,5},{5,6},{6,7},{7,8},{8,9},{9,10},{10,1... | collective-permute-start | bytes 393224 | tf_op jit(solution)/shard_map/while/body/eval_jaxpr/ppermute | solution.py:16
  141.5 12.8 %collective-permute-start = (bf16[32,2048]{1,0:T(8,128)(2,1)S(1)}, bf16[32,2048]{1,0:T(8,128)(2,1)S(1)}, u32[]{:S(2)}, u32[]{:S(2)}) collective-permute-start(bf16[32,2048]{1,0:T(8,128)(2,1)S(1)} %get-tuple-element.433), channel_id=1, source_target_pairs={{0,1},{1,2},{2,3},{3,4},{4,5},{5,6},{6,7},{7,8},{8,9},{9,10},{10,1... | collective-permute-start | bytes 393224 | tf_op jit(solution)/shard_map/while/body/eval_jaxpr/ppermute | solution.py:16
  155.0 6.3 %collective-permute-start = (bf16[32,2048]{1,0:T(8,128)(2,1)S(1)}, bf16[32,2048]{1,0:T(8,128)(2,1)S(1)}, u32[]{:S(2)}, u32[]{:S(2)}) collective-permute-start(bf16[32,2048]{1,0:T(8,128)(2,1)S(1)} %get-tuple-element.433), channel_id=1, source_target_pairs={{0,1},{1,2},{2,3},{3,4},{4,5},{5,6},{6,7},{7,8},{8,9},{9,10},{10,1... | collective-permute-start | bytes 393224 | tf_op jit(solution)/shard_map/while/body/eval_jaxpr/ppermute | solution.py:16
  162.0 8.2 %collective-permute-start = (bf16[32,2048]{1,0:T(8,128)(2,1)S(1)}, bf16[32,2048]{1,0:T(8,128)(2,1)S(1)}, u32[]{:S(2)}, u32[]{:S(2)}) collective-permute-start(bf16[32,2048]{1,0:T(8,128)(2,1)S(1)} %get-tuple-element.433), channel_id=1, source_target_pairs={{0,1},{1,2},{2,3},{3,4},{4,5},{5,6},{6,7},{7,8},{8,9},{9,10},{10,1... | collective-permute-start | bytes 393224 | tf_op jit(solution)/shard_map/while/body/eval_jaxpr/ppermute | solution.py:16
  170.9 7.2 %collective-permute-start = (bf16[32,2048]{1,0:T(8,128)(2,1)S(1)}, bf16[32,2048]{1,0:T(8,128)(2,1)S(1)}, u32[]{:S(2)}, u32[]{:S(2)}) collective-permute-start(bf16[32,2048]{1,0:T(8,128)(2,1)S(1)} %get-tuple-element.433), channel_id=1, source_target_pairs={{0,1},{1,2},{2,3},{3,4},{4,5},{5,6},{6,7},{7,8},{8,9},{9,10},{10,1... | collective-permute-start | bytes 393224 | tf_op jit(solution)/shard_map/while/body/eval_jaxpr/ppermute | solution.py:16
  178.8 13.7 %collective-permute-start = (bf16[32,2048]{1,0:T(8,128)(2,1)S(1)}, bf16[32,2048]{1,0:T(8,128)(2,1)S(1)}, u32[]{:S(2)}, u32[]{:S(2)}) collective-permute-start(bf16[32,2048]{1,0:T(8,128)(2,1)S(1)} %get-tuple-element.433), channel_id=1, source_target_pairs={{0,1},{1,2},{2,3},{3,4},{4,5},{5,6},{6,7},{7,8},{8,9},{9,10},{10,1... | collective-permute-start | bytes 393224 | tf_op jit(solution)/shard_map/while/body/eval_jaxpr/ppermute | solution.py:16
  193.2 7.2 %collective-permute-start = (bf16[32,2048]{1,0:T(8,128)(2,1)S(1)}, bf16[32,2048]{1,0:T(8,128)(2,1)S(1)}, u32[]{:S(2)}, u32[]{:S(2)}) collective-permute-start(bf16[32,2048]{1,0:T(8,128)(2,1)S(1)} %get-tuple-element.433), channel_id=1, source_target_pairs={{0,1},{1,2},{2,3},{3,4},{4,5},{5,6},{6,7},{7,8},{8,9},{9,10},{10,1... | collective-permute-start | bytes 393224 | tf_op jit(solution)/shard_map/while/body/eval_jaxpr/ppermute | solution.py:16
  201.1 7.2 %collective-permute-start = (bf16[32,2048]{1,0:T(8,128)(2,1)S(1)}, bf16[32,2048]{1,0:T(8,128)(2,1)S(1)}, u32[]{:S(2)}, u32[]{:S(2)}) collective-permute-start(bf16[32,2048]{1,0:T(8,128)(2,1)S(1)} %get-tuple-element.433), channel_id=1, source_target_pairs={{0,1},{1,2},{2,3},{3,4},{4,5},{5,6},{6,7},{7,8},{8,9},{9,10},{10,1... | collective-permute-start | bytes 393224 | tf_op jit(solution)/shard_map/while/body/eval_jaxpr/ppermute | solution.py:16
  209.0 7.2 %collective-permute-start = (bf16[32,2048]{1,0:T(8,128)(2,1)S(1)}, bf16[32,2048]{1,0:T(8,128)(2,1)S(1)}, u32[]{:S(2)}, u32[]{:S(2)}) collective-permute-start(bf16[32,2048]{1,0:T(8,128)(2,1)S(1)} %get-tuple-element.433), channel_id=1, source_target_pairs={{0,1},{1,2},{2,3},{3,4},{4,5},{5,6},{6,7},{7,8},{8,9},{9,10},{10,1... | collective-permute-start | bytes 393224 | tf_op jit(solution)/shard_map/while/body/eval_jaxpr/ppermute | solution.py:16
  216.9 7.6 %collective-permute-start = (bf16[32,2048]{1,0:T(8,128)(2,1)S(1)}, bf16[32,2048]{1,0:T(8,128)(2,1)S(1)}, u32[]{:S(2)}, u32[]{:S(2)}) collective-permute-start(bf16[32,2048]{1,0:T(8,128)(2,1)S(1)} %get-tuple-element.433), channel_id=1, source_target_pairs={{0,1},{1,2},{2,3},{3,4},{4,5},{5,6},{6,7},{7,8},{8,9},{9,10},{10,1... | collective-permute-start | bytes 393224 | tf_op jit(solution)/shard_map/while/body/eval_jaxpr/ppermute | solution.py:16
  225.2 7.2 %collective-permute-start = (bf16[32,2048]{1,0:T(8,128)(2,1)S(1)}, bf16[32,2048]{1,0:T(8,128)(2,1)S(1)}, u32[]{:S(2)}, u32[]{:S(2)}) collective-permute-start(bf16[32,2048]{1,0:T(8,128)(2,1)S(1)} %get-tuple-element.433), channel_id=1, source_target_pairs={{0,1},{1,2},{2,3},{3,4},{4,5},{5,6},{6,7},{7,8},{8,9},{9,10},{10,1... | collective-permute-start | bytes 393224 | tf_op jit(solution)/shard_map/while/body/eval_jaxpr/ppermute | solution.py:16
  233.2 7.2 %collective-permute-start = (bf16[32,2048]{1,0:T(8,128)(2,1)S(1)}, bf16[32,2048]{1,0:T(8,128)(2,1)S(1)}, u32[]{:S(2)}, u32[]{:S(2)}) collective-permute-start(bf16[32,2048]{1,0:T(8,128)(2,1)S(1)} %get-tuple-element.433), channel_id=1, source_target_pairs={{0,1},{1,2},{2,3},{3,4},{4,5},{5,6},{6,7},{7,8},{8,9},{9,10},{10,1... | collective-permute-start | bytes 393224 | tf_op jit(solution)/shard_map/while/body/eval_jaxpr/ppermute | solution.py:16
  241.1 7.2 %collective-permute-start = (bf16[32,2048]{1,0:T(8,128)(2,1)S(1)}, bf16[32,2048]{1,0:T(8,128)(2,1)S(1)}, u32[]{:S(2)}, u32[]{:S(2)}) collective-permute-start(bf16[32,2048]{1,0:T(8,128)(2,1)S(1)} %get-tuple-element.433), channel_id=1, source_target_pairs={{0,1},{1,2},{2,3},{3,4},{4,5},{5,6},{6,7},{7,8},{8,9},{9,10},{10,1... | collective-permute-start | bytes 393224 | tf_op jit(solution)/shard_map/while/body/eval_jaxpr/ppermute | solution.py:16
  249.0 8.6 %collective-permute-start = (bf16[32,2048]{1,0:T(8,128)(2,1)S(1)}, bf16[32,2048]{1,0:T(8,128)(2,1)S(1)}, u32[]{:S(2)}, u32[]{:S(2)}) collective-permute-start(bf16[32,2048]{1,0:T(8,128)(2,1)S(1)} %get-tuple-element.433), channel_id=1, source_target_pairs={{0,1},{1,2},{2,3},{3,4},{4,5},{5,6},{6,7},{7,8},{8,9},{9,10},{10,1... | collective-permute-start | bytes 393224 | tf_op jit(solution)/shard_map/while/body/eval_jaxpr/ppermute | solution.py:16
  257.5 77.2 %copy-start = (f32[1,224,2048]{2,1,0:T(8,128)}, f32[1,224,2048]{2,1,0:T(8,128)S(1)}, u32[]{:S(2)}) copy-start(f32[1,224,2048]{2,1,0:T(8,128)S(1)} %get-tuple-element.273) | copy-start | bytes 5505028
where the time goes:
time: 336 us; the launch traced here: 335 us
  starting transfers between devices  146 us (43%)
  blocking collectives  76.6 us (23%)
  matrix products  61.3 us (18%)
  other arithmetic  24.4 us (7%)
  waiting for transfers between devices  21.1 us (6%)
    ppermute x23, starting transfers between devices, shifted(): lax.ppermute(value, axis, [(source, source + steps) for source in range(i...  146 us
    psum x1, blocking collectives, per_device(): log_scale = lax.psum(local_log, 'tm') / (tm_count * local_slices - 1)  76.6 us
    dot_general x7, matrix products, push_forward(): jnp.dot(weighted, kernel, preferred_element_type=jnp.float32)  35.2 us
    dot_general x4, matrix products, one_block(): lax.dot_general(segment, target, (((0,), (0,)), ((), ())), precision=lax....  26.1 us
    ppermute x23, waiting for transfers between devices, shifted(): lax.ppermute(value, axis, [(source, source + steps) for source in range(i...  21.1 us
    convert_element_type x22, other arithmetic, per_device(): (jnp.arange(point_count, dtype=jnp.int32)[None, :] < supports[:, None]).a...  14.4 us
    convert_element_type x7, other arithmetic, section(): outgoing = (message * block_pot[local_slices - 1]).astype(jnp.bfloat16)  7.46 us
  transfers between devices with their start and end apart: 23, of which 22 were waited for; matrix products, arithmetic and copies ran while one was open for 0% of the time, Pallas kernels for 0%

commit v1 on v0

v1 whole, which is shorter than its diff:
```python
import functools
import math

import jax
import jax.numpy as jnp
from jax import lax
from jax.experimental import pallas as pl
from jax.experimental.pallas import tpu as pltpu
from jax.sharding import PartitionSpec as P

A_DECAY = 0.8
EPS_SCALE = 0.05
LIVE = 1024
TEAM = 8
BLOCK = 32
LOGS = 128
SUP = 8
DEAD = -1e30

F32 = jnp.float32
BF16 = jnp.bfloat16
VMEM = pl.BlockSpec(memory_space=pltpu.VMEM)


def params(mib, grid=False):
    semantics = ("arbitrary",) if grid else None
    return pltpu.CompilerParams(vmem_limit_bytes=mib << 20, dimension_semantics=semantics)


def block_of(device):
    return (device & 1) * 4 + (device >> 1)


def split2(value):
    high = value.astype(BF16)
    return high, (value - high.astype(F32)).astype(BF16)


def split3(value):
    high = value.astype(BF16).astype(F32)
    rest = value - high
    middle = rest.astype(BF16).astype(F32)
    return high, middle, rest - middle


def rows_of(parts):
    width = parts[0].shape[1]
    filler = jnp.zeros((16 - len(parts), width), F32)
    return jnp.concatenate([*parts, filler], axis=0).astype(BF16)


def source_features(points):
    unit = math.log2(math.e) / (2.0 * EPS_SCALE * points.shape[0])
    high, low = split2(points * (2.0 * A_DECAY * unit))
    square = jnp.sum(points * points, axis=0, keepdims=True) * (-A_DECAY * A_DECAY * unit)
    one = jnp.ones_like(square)
    return jnp.concatenate([high, high, low, rows_of((*split3(square), one, one, one))], axis=0)


def target_features(points, support, first=0):
    unit = math.log2(math.e) / (2.0 * EPS_SCALE * points.shape[0])
    high, low = split2(points)
    square = jnp.sum(points * points, axis=0, keepdims=True) * (-unit)
    one = jnp.ones_like(square)
    place = lax.broadcasted_iota(jnp.int32, square.shape, 1).astype(F32) + first
    live = place < support
    top, middle, rest = split3(square)
    top = jnp.where(live, top, DEAD)
    middle = jnp.where(live, middle, 0.0)
    rest = jnp.where(live, rest, 0.0)
    return jnp.concatenate([high, low, high, rows_of((one, one, one, top, middle, rest))], axis=0)


def fill_kernel(source, target, support, turned, features, write, first=0):
    turned[...] = source_features(source).T
    features[...] = target_features(target, support, first)
    step = 256
    for start in range(0, source.shape[1], step):
        exponent = jnp.dot(
            turned[start : start + step, :], features[...], preferred_element_type=F32
        )
        write(start, step, jnp.exp2(exponent).astype(BF16))


def log_lanes(logs):
    lane = lax.broadcasted_iota(jnp.int32, (logs.shape[0], LOGS), 1)
    high, middle, rest = split3(logs)
    third = jnp.where(lane == 2, rest, 0.0)
    return jnp.where(lane == 0, high, jnp.where(lane == 1, middle, third)).astype(BF16)


def first_step(own_ref, other_ref, pot_own, pot_other, sup_ref, *refs):
    outs, message_ref, source, target, pot_first, pot_next, turned, features, kernel = (
        refs[:4],
        *refs[4:],
    )
    position = lax.axis_index("tm")

    @pl.when(position == 0)
    def _():
        source[...] = own_ref[...]
        target[...] = other_ref[:, :LIVE]
        pot_first[...] = pot_own[...]
        pot_next[...] = pot_other[:, :LIVE]

    @pl.when(position == 1)
    def _():
        source[...] = other_ref[...]
        target[...] = own_ref[:, :LIVE]
        pot_first[...] = pot_other[...]
        pot_next[...] = pot_own[:, :LIVE]

    @pl.when(position < 2)
    def _():
        support = sup_ref[0]

        def write(start, size, values):
            kernel[start : start + size, :] = values

        fill_kernel(source[...], target[...], support, turned, features, write)
        pushed = jnp.dot(pot_first[...], kernel[...], preferred_element_type=F32)
        total = jnp.sum(pushed, axis=1, keepdims=True)
        message = pushed * (support / total)
        message_ref[...] = message.astype(BF16)
        weighted = (message * pot_next[...].astype(F32)).astype(BF16)
        logs = log_lanes(jnp.log(total / support))
        for index, out in enumerate(outs):
            rows = slice(index * BLOCK, (index + 1) * BLOCK)
            out[:, :LIVE] = weighted[rows]
            out[:, LIVE:] = logs[rows]


def split_pots(pot_ref, *outs):
    device = lax.axis_index("tm") % TEAM
    last = pot_ref.shape[0] // BLOCK - 1
    for mask, out in enumerate(outs):
        row = pl.multiple_of(jnp.minimum(block_of(device ^ mask), last) * BLOCK, BLOCK)
        out[...] = pot_ref[pl.ds(row, BLOCK), :].astype(BF16)


def build(last_position, *refs):
    slots, tail_ref = refs[:TEAM], refs[TEAM]
    kernel_ref, seventh_ref, sup_ref, sums_ref = refs[TEAM + 1 : TEAM + 5]
    points, turned, features = refs[TEAM + 5 :]
    position = lax.axis_index("tm")
    device, team = position % TEAM, position // TEAM
    last_team = last_position // TEAM
    dims = tail_ref.shape[0]
    step = pl.program_id(0)

    @pl.when(step == 0)
    def _():
        for mask, slot in enumerate(slots):
            points[device ^ mask] = slot[...]
        for index in range(TEAM):
            sup_ref[index : index + 1, :] = points[index, dims : dims + 1, :LOGS]
        seventh_ref[...] = points[TEAM - 1]
        sums_ref[...] = jnp.zeros_like(sums_ref)

    def write(start, size, values):
        kernel_ref[0, start : start + size, :] = values

    inner = (step < TEAM - 1) & ((team > 0) | (step > 1)) & (step > 0)
    closing = (step == TEAM - 1) & ((team < last_team) | (position == last_position))

    @pl.when(inner | closing)
    def _():
        fill_kernel(
            points[step - 1, :dims, :],
            points[step, :dims, :],
            points[step, dims, 0],
            turned,
            features,
            write,
        )

    @pl.when((step == TEAM) & (position == last_position))
    def _():
        fill_kernel(
            points[TEAM - 2, :dims, :],
            tail_ref[...],
            points[TEAM - 1, dims, 0],
            turned,
            features,
            write,
            first=LIVE,
        )

    @pl.when((step >= TEAM - 1) & (position == last_position))
    def _():
        one = jnp.ones((8, LIVE), BF16)
        sums_ref[...] += lax.dot_general(
            one, kernel_ref[0], (((1,), (1,)), ((), ())), preferred_element_type=F32
        )


def bridge(before_ref, start_ref, kernel_ref, turned, features):
    @pl.when(lax.axis_index("tm") >= TEAM)
    def _():
        def write(start, size, values):
            kernel_ref[start : start + size, :] = values

        dims = before_ref.shape[0] - SUP
        fill_kernel(
            before_ref[:dims, :],
            start_ref[:dims, :],
            start_ref[dims, 0],
            turned,
            features,
            write,
        )


def sweep(stage, last_team, carried, arrivals, flag_ref, *refs):
    refs = list(refs)

    def take(count):
        taken = refs[:count]
        del refs[:count]
        return taken

    kernel_ref, opening_ref, sup_ref, sums_ref = take(4)
    pots = take(TEAM)
    incoming = take(arrivals)
    previous = take(TEAM if carried else 0)
    outs = take(TEAM)
    (leave_ref,) = take(1)
    weighted, logs, pot_all, stored = refs
    position = lax.axis_index("tm")
    device, team = position % TEAM, position // TEAM
    step = pl.program_id(0)
    first = 0 if stage else 2
    final = TEAM - 2 if stage == last_team else TEAM - 1
    active = team == stage

    @pl.when(active & (step == first))
    def _():
        for mask, pot in enumerate(pots):
            pot_all[device ^ mask] = pot[...]

        def load(ref):
            weighted[...] = ref[:, :LIVE]
            total = jnp.sum(ref[:, LIVE:].astype(F32), axis=1, keepdims=True)
            logs[...] = jnp.broadcast_to(total, logs.shape)

        if arrivals == 1:
            load(incoming[0])
        else:
            for index, ref in enumerate(incoming):
                pl.when(device >> 1 == index)(functools.partial(load, ref))

    def advance(kernel):
        support = sup_ref[pl.ds(step, 1), 0:1]
        pushed = jnp.dot(weighted[...], kernel, preferred_element_type=F32)
        total = jnp.sum(pushed, axis=1, keepdims=True)
        message = pushed * (support / total)
        stored[step] = message.astype(BF16)
        weighted[...] = (message * pot_all[step].astype(F32)).astype(BF16)
        logs[...] += jnp.log(total / support)

    if stage:
        pl.when(active & (step == 0))(lambda: advance(opening_ref[...]))
    inner = (step >= max(first, 1)) & (step <= final)
    pl.when(active & inner)(lambda: advance(kernel_ref[0]))

    @pl.when(active & (step == TEAM - 1))
    def _():
        if stage == last_team:
            support = sup_ref[TEAM - 1 : TEAM, 0:1]
            reach = jnp.sum(
                weighted[...].astype(F32) * sums_ref[0:1, :], axis=1, keepdims=True
            )
            logs[...] += jnp.log(reach / support)
            stored[TEAM - 1] = weighted[...]
        lanes = log_lanes(logs[:, 0:1])
        for mask, out in enumerate(outs):
            out[:, :LIVE] = stored[device ^ mask]
            out[:, LIVE:] = lanes
        leave_ref[:, :LIVE] = weighted[...]
        leave_ref[:, LIVE:] = lanes

    if carried:

        @pl.when((team != stage) & (step == TEAM - 1))
        def _():
            for source, out in zip(previous, outs):
                out[...] = source[...]


def gather_logs(scale, *refs):
    blocks, out_ref, column = refs[:TEAM], refs[TEAM], refs[TEAM + 1]
    device = lax.axis_index("tm") % TEAM
    for mask, block in enumerate(blocks):
        total = jnp.sum(block[...].astype(F32), axis=1, keepdims=True) * scale
        row = pl.multiple_of(block_of(device ^ mask) * BLOCK, BLOCK)
        column[pl.ds(row, BLOCK), :] = jnp.broadcast_to(total, (BLOCK, LOGS))
    out_ref[...] = column[...].T[0:8, :]


def finish(last_position, *refs):
    blocks = refs[:TEAM]
    early_own, early_other, sup_ref, kernel_ref, out_ref, weighted, halves, sem = refs[TEAM:]
    position = lax.axis_index("tm")
    device = position % TEAM
    spare = out_ref.shape[1] - LIVE
    columns = out_ref.shape[0]

    @pl.when(position == 0)
    def _():
        place = lax.broadcasted_iota(jnp.int32, out_ref.shape, 1)
        out_ref[...] = jnp.where(place < sup_ref[0], 1.0, 0.0)

    @pl.when(position == 1)
    def _():
        cut = 4 * BLOCK
        out_ref[:cut, :LIVE] = early_other[...].astype(F32)
        out_ref[cut:, :LIVE] = early_own[: columns - cut, :].astype(F32)
        out_ref[:, LIVE:] = jnp.zeros((columns, spare), F32)

    @pl.when((position > 1) & (position < last_position))
    def _():
        for mask, block in enumerate(blocks):

            @pl.when(device ^ mask < TEAM - 1)
            def _():
                row = pl.multiple_of(block_of(device ^ mask) * BLOCK, BLOCK)
                out_ref[pl.ds(row, BLOCK), :LIVE] = block[:, :LIVE].astype(F32)

        out_ref[:, LIVE:] = jnp.zeros((columns, spare), F32)

    @pl.when(position == last_position)
    def _():
        copies = []
        for half in range(2):
            copy = pltpu.make_async_copy(
                kernel_ref.at[TEAM - 1 + half], halves.at[half], sem.at[half]
            )
            copy.start()
            copies.append(copy)
        for mask in range(1, TEAM):
            row = block_of(TEAM - 1 - mask) * BLOCK
            weighted[row : row + BLOCK, :] = blocks[mask][:, :LIVE]
        total = jnp.zeros((columns, 1), F32)
        for half, copy in enumerate(copies):
            copy.wait()
            pushed = jnp.dot(weighted[...], halves[half], preferred_element_type=F32)
            out_ref[:, half * LIVE : (half + 1) * LIVE] = pushed
            total = total + jnp.sum(pushed, axis=1, keepdims=True)
        ratio = sup_ref[0].astype(F32) / total
        out_ref[...] = out_ref[...] * ratio


def shape(*dims, dtype=BF16):
    return jax.ShapeDtypeStruct(dims, dtype)


def scratch(*dims, dtype=BF16):
    return pltpu.VMEM(dims, dtype)


def per_device(points, potentials, supports):
    points, potentials = points[0], potentials[0]
    dims, count = points.shape
    columns = potentials.shape[0]
    devices = lax.axis_size("tm")
    position = lax.axis_index("tm")
    last = devices - 1
    teams = devices // TEAM
    depth = 3 * dims + 16
    smem = pl.BlockSpec(memory_space=pltpu.SMEM)
    anywhere = pl.BlockSpec(memory_space=pl.ANY)

    def move(value, pairs):
        return lax.ppermute(value, "tm", pairs)

    def swap(value, mask, keep=lambda source, target: True):
        pairs = [(i, i ^ mask) for i in range(devices) if keep(i, i ^ mask)]
        return move(value, pairs)

    other_points = move(points, [(0, 1), (1, 0)])
    first_support = move(supports, [(1, 0)])
    half = 4 * BLOCK
    padded = jnp.pad(potentials, ((0, 2 * half - columns), (0, 0)), constant_values=1.0)
    mine = jnp.where(position == 1, half, 0)
    own_pots = lax.dynamic_slice_in_dim(padded, mine, half, 0).astype(BF16)
    sent_pots = lax.dynamic_slice_in_dim(padded, half - mine, half, 0).astype(BF16)
    other_pots = move(sent_pots, [(0, 1), (1, 0)])

    payload = jnp.concatenate(
        [points[:, :LIVE], jnp.broadcast_to(supports.astype(F32), (SUP, LIVE))], axis=0
    ).astype(jnp.float16)
    far = [payload] + [swap(payload, mask) for mask in (2, 4, 6)]

    pots = pl.pallas_call(
        split_pots,
        grid=(1,),
        out_shape=[shape(BLOCK, LIVE)] * TEAM,
        in_specs=[pl.BlockSpec((columns, LIVE), lambda i: (0, 0))],
        out_specs=[pl.BlockSpec((BLOCK, LIVE), lambda i: (0, 0))] * TEAM,
        compiler_params=params(16),
        name="pots",
    )(potentials)

    def holds(source, target):
        return 2 <= source < last and target % TEAM != TEAM - 1

    pots = [pots[0]] + [swap(pots[mask], mask, holds) for mask in range(1, TEAM)]

    support_one = jnp.where(position == 1, supports, first_support).astype(F32)
    *opened, early = pl.pallas_call(
        first_step,
        out_shape=[shape(BLOCK, LIVE + LOGS)] * 4 + [shape(half, LIVE)],
        in_specs=[VMEM, VMEM, VMEM, VMEM, smem],
        out_specs=[VMEM] * 5,
        scratch_shapes=[
            scratch(dims, count, dtype=F32),
            scratch(dims, LIVE, dtype=F32),
            scratch(half, count),
            scratch(half, LIVE),
            scratch(count, depth),
            scratch(depth, LIVE),
            scratch(count, LIVE),
        ],
        compiler_params=params(24),
        name="first",
    )(points, other_points, own_pots, other_pots, support_one)
    early_other = move(early, [(0, 1)])
    arrived = [opened[0]]
    for index in range(1, 4):
        pairs = [(c, c + 2 * index) for c in range(2) if c + 2 * index < TEAM - 1]
        arrived.append(move(opened[index], pairs))

    near = [swap(value, 1) for value in far]
    slots = [None] * TEAM
    for index, mask in enumerate((0, 2, 4, 6)):
        slots[mask] = far[index].astype(F32)
        slots[mask + 1] = near[index].astype(F32)

    full = pl.BlockSpec((dims + SUP, LIVE), lambda i: (0, 0))
    kernels, seventh, team_sup, sums = pl.pallas_call(
        functools.partial(build, last),
        grid=(TEAM + 1,),
        out_shape=[
            shape(TEAM + 1, LIVE, LIVE),
            shape(dims + SUP, LIVE, dtype=F32),
            shape(TEAM, LOGS, dtype=F32),
            shape(8, LIVE, dtype=F32),
        ],
        in_specs=[full] * TEAM + [pl.BlockSpec((dims, LIVE), lambda i: (0, 1))],
        out_specs=[
            pl.BlockSpec((1, LIVE, LIVE), lambda i: (i, 0, 0)),
            full,
            pl.BlockSpec((TEAM, LOGS), lambda i: (0, 0)),
            pl.BlockSpec((8, LIVE), lambda i: (0, 0)),
        ],
        scratch_shapes=[
            scratch(TEAM, dims + SUP, LIVE, dtype=F32),
            scratch(LIVE, depth),
            scratch(depth, LIVE),
        ],
        compiler_params=params(24, True),
        name="build",
    )(*slots, points)

    def run_sweep(stage, opening, sums, incoming, previous):
        flag = (position // TEAM == stage).astype(jnp.int32).reshape(1)
        low, high = (2, TEAM - 1) if stage == 0 else (1, TEAM - 1)

        def kernel_at(i, flag):
            return (jnp.where(flag[0] == 1, jnp.clip(i, low, high), low), 0, 0)

        def whole(*dims):
            return pl.BlockSpec(dims, lambda i, flag: (0,) * len(dims))

        wide = whole(BLOCK, LIVE + LOGS)
        return pl.pallas_call(
            functools.partial(sweep, stage, teams - 1, previous is not None, len(incoming)),
            grid_spec=pltpu.PrefetchScalarGridSpec(
                num_scalar_prefetch=1,
                grid=(TEAM,),
                in_specs=[
                    pl.BlockSpec((1, LIVE, LIVE), kernel_at),
                    whole(LIVE, LIVE) if stage else whole(8, LIVE),
                    whole(TEAM, LOGS),
                    whole(8, LIVE),
                ]
                + [whole(BLOCK, LIVE)] * TEAM
                + [wide] * len(incoming)
                + [wide] * (TEAM if previous is not None else 0),
                out_specs=[wide] * (TEAM + 1),
                scratch_shapes=[
                    scratch(BLOCK, LIVE),
                    scratch(BLOCK, LOGS, dtype=F32),
                    scratch(TEAM, BLOCK, LIVE),
                    scratch(TEAM, BLOCK, LIVE),
                ],
            ),
            out_shape=[shape(BLOCK, LIVE + LOGS)] * (TEAM + 1),
            compiler_params=params(24, True),
            name="sweep%d" % min(stage, 1),
        )(flag, kernels, opening, team_sup, sums, *pots, *incoming, *(previous or []))

    before = move(
        seventh.astype(jnp.float16), [(i, i + TEAM) for i in range(devices - TEAM)]
    ).astype(F32)
    *blocks, leaving = run_sweep(0, sums, sums, arrived, None)

    for stage in range(1, teams):
        base = stage * TEAM
        incoming = move(leaving, [(base - TEAM + i, base + i) for i in range(TEAM - 1)])
        if stage == 1:
            before, sums, leaving = lax.optimization_barrier((before, sums, leaving))
            opening = pl.pallas_call(
                bridge,
                out_shape=shape(LIVE, LIVE),
                in_specs=[VMEM, VMEM],
                out_specs=VMEM,
                scratch_shapes=[scratch(LIVE, depth), scratch(depth, LIVE)],
                compiler_params=params(16),
                name="bridge",
            )(before, start_of(slots, position))
            top = devices - TEAM
            for mask in (4, 2, 1):
                sources = [i for i in range(TEAM) if i % (2 * mask) == 2 * mask - 1]
                sums = sums + move(sums, [(top + i, top + i - mask) for i in sources])
        *blocks, leaving = run_sweep(stage, opening, sums, [incoming], blocks)

    def ready(source, target):
        return source % TEAM != TEAM - 1 and target > 1

    blocks = [blocks[0]] + [swap(blocks[mask], mask, ready) for mask in range(1, TEAM)]
    lanes = pl.BlockSpec((BLOCK, LOGS), lambda i: (0, LIVE // LOGS))
    logs = pl.pallas_call(
        functools.partial(gather_logs, 1.0 / last),
        grid=(1,),
        out_shape=shape(8, TEAM * BLOCK, dtype=F32),
        in_specs=[lanes] * TEAM,
        out_specs=pl.BlockSpec((8, TEAM * BLOCK), lambda i: (0, 0)),
        scratch_shapes=[scratch(TEAM * BLOCK, LOGS, dtype=F32)],
        compiler_params=params(16),
        name="logs",
    )(*blocks)
    for team in range(teams - 1):
        shift = (teams - 1 - team) * TEAM
        moved = move(logs, [(devices - TEAM + i, devices - TEAM + i - shift) for i in range(TEAM)])
        logs = jnp.where(position // TEAM == team, moved, logs)
    log_scale = logs[0, :columns]

    messages = pl.pallas_call(
        functools.partial(finish, last),
        out_shape=shape(columns, count, dtype=F32),
        in_specs=[VMEM] * (TEAM + 2) + [smem, anywhere],
        out_specs=VMEM,
        scratch_shapes=[
            scratch(columns, LIVE),
            scratch(2, LIVE, LIVE),
            pltpu.SemaphoreType.DMA((2,)),
        ],
        compiler_params=params(24),
        name="finish",
    )(*blocks, early, early_other, supports, kernels)
    return messages[None], log_scale


def start_of(slots, position):
    device = position % TEAM
    value = slots[0]
    for mask in range(1, TEAM):
        value = jnp.where(device == mask, slots[mask], value)
    return value


def solution(mesh):
    whole = P(("groups", "tm"), None, None)
    return jax.shard_map(
        per_device,
        mesh=mesh,
        in_specs=(whole, whole, P(("groups", "tm"))),
        out_specs=(whole, P("groups")),
        check_vma=False,
    )
```

time: 336 us -> 121 us (0.36)
  starting transfers between devices: 146 us -> 50.6 us
  blocking collectives: 76.6 us -> 0 us
  matrix products: 61.3 us -> 0 us
  other arithmetic: 24.4 us -> 1.06 us
  local copies, waits for them, and re-layouts: 2.04 us -> 20.8 us
  Pallas kernels: 0 us -> 14.6 us
  waiting for transfers between devices: 21.1 us -> 29.9 us
    ppermute x23 -> x34, starting transfers between devices: 146 us -> 50.6 us  [move(): return lax.ppermute(value, 'tm', pairs)]
    psum x1 -> x0, blocking collectives: 76.6 us -> none  [per_device(): log_scale = lax.psum(local_log, 'tm') / (tm_count * local_slices - 1)]
    dot_general x11 -> x0, matrix products: 61.3 us -> none  [the longest x7 35.2 us: push_forward(): jnp.dot(weighted, kernel, preferred_element_type=jnp.float32)]
    convert_element_type x29 -> x9, other arithmetic: 21.9 us -> 0.19 us  [the longest x4 0.09 us: per_device(): slots[mask + 1] = near[index].astype(F32)]
    unnamed x2 -> x10, local copies, waits for them, and re-layouts: 0.01 us -> 19.2 us
    pallas_call x0 -> x8, Pallas kernels: none -> 14.6 us  [the longest x1 5.56 us: per_device(): pl.pallas_call(functools.partial(build, last), grid=(TEAM + 1,), out_shap...]
    ppermute x23 -> x34, waiting for transfers between devices: 21.1 us -> 29.9 us  [move(): return lax.ppermute(value, 'tm', pairs)]
  transfers between devices with their start and end apart: 23 -> 34, of which waited for: 22 -> 10; matrix products, arithmetic and copies ran while one was open for 0% -> 1% of each run, Pallas kernels for 0% -> 7%
where the time goes in v1:
time: 121 us; the launch traced here: 119 us
  starting transfers between devices  50.6 us (42%)
  waiting for transfers between devices  29.9 us (25%)
  local copies, waits for them, and re-layouts  20.8 us (17%)
  Pallas kernels  14.6 us (12%)
  between operations  2.54 us (2%)
    ppermute x34, starting transfers between devices, move(): return lax.ppermute(value, 'tm', pairs)  50.6 us
    ppermute x34, waiting for transfers between devices, move(): return lax.ppermute(value, 'tm', pairs)  29.9 us
    unnamed x10, local copies, waits for them, and re-layouts  19.2 us
    pallas_call x1, Pallas kernels, per_device(): pl.pallas_call(functools.partial(build, last), grid=(TEAM + 1,), out_shap...  5.56 us
    pallas_call x2, Pallas kernels, run_sweep(): pl.pallas_call(functools.partial(sweep, stage, teams - 1, previous is not...  5.06 us
  transfers between devices with their start and end apart: 34, of which 10 were waited for; matrix products, arithmetic and copies ran while one was open for 1% of the time, Pallas kernels for 7%

profile of v1, /device:TPU:0, one launch (start us, length us, event | category | flops | bytes accessed | tf_op | source)
XLA Modules:
  0.0 119.4 jit_solution(17382654611280755475)
XLA Ops:
  0.6 1.6 %fusion.1 = (bf16[128,2048]{1,0:T(8,128)(2,1)S(1)}, bf16[128,2048]{1,0:T(8,128)(2,1)S(1)}) fusion(s32[]{:T(128)S(6)} %select_n.83, f32[224,2048]{1,0:T(8,128)} %bitcast.8, s32[]{:T(128)S(6)} %select_n.82), kind=kLoop, calls=%fused_computation.3 | loop fusion | bytes 2883592 | tf_op jit(solution)/shard_map/convert_element_type | solution.py:386
  2.3 2.4 %collective-permute-start.16 = (bf16[128,2048]{1,0:T(8,128)(2,1)S(1)}, bf16[128,2048]{1,0:T(8,128)(2,1)S(1)}, u32[]{:S(2)}, u32[]{:S(2)}) collective-permute-start(bf16[128,2048]{1,0:T(8,128)(2,1)S(1)} %get-tuple-element.74), channel_id=1, source_target_pairs={{0,1},{1,0},{16,17},{17,16}} | collective-permute-start | bytes 1572872 | tf_op jit(solution)/shard_map/ppermute | solution.py:374
  5.4 1.4 %collective-permute-start.1 = (f16[72,1024]{1,0:T(8,128)(2,1)S(1)}, f16[72,1024]{1,0:T(8,128)(2,1)S(1)}, u32[]{:S(2)}, u32[]{:S(2)}) collective-permute-start(f16[72,1024]{1,0:T(8,128)(2,1)S(1)} %get-tuple-element.76), channel_id=1, source_target_pairs={{0,2},{1,3},{2,0},{3,1},{4,6},{5,7},{6,4},{7,5},{8,10},{9,11},{10,... | collective-permute-start | bytes 442376 | tf_op jit(solution)/shard_map/ppermute | solution.py:374
  6.8 1.9 %collective-permute-start.15 = (f32[64,2048]{1,0:T(8,128)S(1)}, f32[64,2048]{1,0:T(8,128)S(1)}, u32[]{:S(2)}, u32[]{:S(2)}) collective-permute-start(f32[64,2048]{1,0:T(8,128)S(1)} %bitcast.11), channel_id=1, source_target_pairs={{0,1},{1,0},{16,17},{17,16}} | collective-permute-start | bytes 1572872 | tf_op jit(solution)/shard_map/ppermute | solution.py:374
  9.7 1.5 %collective-permute-done.1 = f16[72,1024]{1,0:T(8,128)(2,1)S(1)} collective-permute-done((f16[72,1024]{1,0:T(8,128)(2,1)S(1)}, f16[72,1024]{1,0:T(8,128)(2,1)S(1)}, u32[]{:S(2)}, u32[]{:S(2)}) %collective-permute-start.1) | collective-permute-done | bytes 147488 | tf_op jit(solution)/shard_map/ppermute | solution.py:374
  11.3 4.2 %collective-permute-done.3 = f16[72,1024]{1,0:T(8,128)(2,1)S(1)} collective-permute-done((f16[72,1024]{1,0:T(8,128)(2,1)S(1)}, f16[72,1024]{1,0:T(8,128)(2,1)S(1)}, u32[]{:S(2)}, u32[]{:S(2)}) %collective-permute-start.3) | collective-permute-done | bytes 147488 | tf_op jit(solution)/shard_map/ppermute | solution.py:374
  18.0 5.6 %build.1 = (bf16[9,1024,1024]{2,1,0:T(8,128)(2,1)S(1)}, f32[72,1024]{1,0:T(8,128)S(1)}, f32[8,128]{1,0:T(8,128)S(1)}, f32[8,1024]{1,0:T(8,128)S(1)}) custom-call(f32[72,1024]{1,0:T(8,128)S(1)} %get-tuple-element.77.refs_0_, f32[72,1024]{1,0:T(8,128)S(1)} %convert_element_type.50.refs_1_, f32[72,1024]{1,0:T(8,128)S(1)} %convert_element_type.51.refs_2_, ...), custom_call_target="tpu_custom_call" | custom-call | tf_op jit(solution)/shard_map/build/pallas_call | solution.py:440
  23.6 6.5 %copy-done = bf16[9,1024,1024]{2,1,0:T(8,128)(2,1)} copy-done((bf16[9,1024,1024]{2,1,0:T(8,128)(2,1)}, bf16[9,1024,1024]{2,1,0:T(8,128)(2,1)S(1)}, u32[]{:S(2)}) %copy-start) | copy-done | bytes 18874392
  30.0 4.1 %collective-permute-start.7 = (f16[72,1024]{1,0:T(8,128)(2,1)S(1)}, f16[72,1024]{1,0:T(8,128)(2,1)S(1)}, u32[]{:S(2)}, u32[]{:S(2)}) collective-permute-start(f16[72,1024]{1,0:T(8,128)(2,1)S(1)} %convert_element_type.57), channel_id=1, source_target_pairs={{0,8},{1,9},{2,10},{3,11},{4,12},{5,13},{6,14},{7,15},{16,24},{17,... | collective-permute-start | bytes 442376 | tf_op jit(solution)/shard_map/ppermute | solution.py:374
  36.9 2.0 %collective-permute-done.17 = s32[1]{0:T(128)} collective-permute-done((s32[1]{0:T(128)}, s32[1]{0:T(128)}, u32[]{:S(2)}, u32[]{:S(2)}) %collective-permute-start.17) | collective-permute-done | bytes 36 | tf_op jit(solution)/shard_map/ppermute | solution.py:374
  44.9 2.2 %first.1 = (bf16[32,1152]{1,0:T(8,128)(2,1)S(1)}, bf16[32,1152]{1,0:T(8,128)(2,1)S(1)}, bf16[32,1152]{1,0:T(8,128)(2,1)S(1)}, bf16[32,1152]{1,0:T(8,128)(2,1)S(1)}, bf16[128,1024]{1,0:T(8,128)(2,1)S(1)}) custom-call(f32[64,2048]{1,0:T(8,128)S(1)} %bitcast.13, f32[64,2048]{1,0:T(8,128)S(1)} %collective-permute-done.15.other_ref, ...), custom_call_target="tpu_custom_call" | custom-call | tf_op jit(solution)/shard_map/first/pallas_call | solution.py:410
  47.1 6.6 %collective-permute-start.18 = (bf16[32,1152]{1,0:T(8,128)(2,1)S(1)}, bf16[32,1152]{1,0:T(8,128)(2,1)S(1)}, u32[]{:S(2)}, u32[]{:S(2)}) collective-permute-start(bf16[32,1152]{1,0:T(8,128)(2,1)S(1)} %get-tuple-element.51), channel_id=1, source_target_pairs={{0,2},{1,3},{16,18},{17,19}} | collective-permute-start | bytes 221192 | tf_op jit(solution)/shard_map/ppermute | solution.py:374
  58.4 4.8 %collective-permute-done.9.refs_6_ = bf16[32,1024]{1,0:T(8,128)(2,1)S(1)} collective-permute-done((bf16[32,1024]{1,0:T(8,128)(2,1)S(1)}, bf16[32,1024]{1,0:T(8,128)(2,1)S(1)}, u32[]{:S(2)}, u32[]{:S(2)}) %collective-permute-start.9) | collective-permute-done | bytes 65568 | tf_op jit(solution)/shard_map/ppermute | solution.py:374
  63.2 6.4 %copy-done.1 = bf16[9,1024,1024]{2,1,0:T(8,128)(2,1)S(1)} copy-done((bf16[9,1024,1024]{2,1,0:T(8,128)(2,1)S(1)}, bf16[9,1024,1024]{2,1,0:T(8,128)(2,1)}, u32[]{:S(2)}) %copy-start.1) | copy-done | bytes 18874392
  69.5 4.4 %sweep0.1 = (bf16[32,1152]{1,0:T(8,128)(2,1)S(1)}, bf16[32,1152]{1,0:T(8,128)(2,1)S(1)}, bf16[32,1152]{1,0:T(8,128)(2,1)S(1)}, bf16[32,1152]{1,0:T(8,128)(2,1)S(...) custom-call(s32[1]{0:T(128)} %bitcast.3.flag_ref, ...), custom_call_target="tpu_custom_call" | custom-call | tf_op jit(solution)/shard_map/sweep0/pallas_call | solution.py:476
  78.6 6.4 %copy-done.2 = bf16[9,1024,1024]{2,1,0:T(8,128)(2,1)S(1)} copy-done((bf16[9,1024,1024]{2,1,0:T(8,128)(2,1)S(1)}, bf16[9,1024,1024]{2,1,0:T(8,128)(2,1)}, u32[]{:S(2)}) %copy-start.2) | copy-done | bytes 18874392
  86.3 3.6 %collective-permute-start.26 = (bf16[32,1152]{1,0:T(8,128)(2,1)S(1)}, bf16[32,1152]{1,0:T(8,128)(2,1)S(1)}, u32[]{:S(2)}, u32[]{:S(2)}) collective-permute-start(bf16[32,1152]{1,0:T(8,128)(2,1)S(1)} %get-tuple-element.67), channel_id=1, source_target_pairs={{0,2},{1,3},{4,6},{5,7},{6,4},{8,10},{9,11},{10,8},{11,9},{12,14},... | collective-permute-start | bytes 221192 | tf_op jit(solution)/shard_map/ppermute | solution.py:374
  89.9 1.3 %collective-permute-start.27 = (bf16[32,1152]{1,0:T(8,128)(2,1)S(1)}, bf16[32,1152]{1,0:T(8,128)(2,1)S(1)}, u32[]{:S(2)}, u32[]{:S(2)}) collective-permute-start(bf16[32,1152]{1,0:T(8,128)(2,1)S(1)} %get-tuple-element.68), channel_id=1, source_target_pairs={{0,3},{1,2},{4,7},{5,6},{6,5},{8,11},{9,10},{10,9},{11,8},{12,15},... | collective-permute-start | bytes 221192 | tf_op jit(solution)/shard_map/ppermute | solution.py:374
  92.5 3.4 %collective-permute-start.29 = (bf16[32,1152]{1,0:T(8,128)(2,1)S(1)}, bf16[32,1152]{1,0:T(8,128)(2,1)S(1)}, u32[]{:S(2)}, u32[]{:S(2)}) collective-permute-start(bf16[32,1152]{1,0:T(8,128)(2,1)S(1)} %get-tuple-element.70), channel_id=1, source_target_pairs={{0,5},{1,4},{2,7},{3,6},{6,3},{8,13},{9,12},{10,15},{11,14},{12,9}... | collective-permute-start | bytes 221192 | tf_op jit(solution)/shard_map/ppermute | solution.py:374
  95.9 2.3 %collective-permute-start.30 = (bf16[32,1152]{1,0:T(8,128)(2,1)S(1)}, bf16[32,1152]{1,0:T(8,128)(2,1)S(1)}, u32[]{:S(2)}, u32[]{:S(2)}) collective-permute-start(bf16[32,1152]{1,0:T(8,128)(2,1)S(1)} %get-tuple-element.71), channel_id=1, source_target_pairs={{0,6},{1,7},{2,4},{3,5},{4,2},{5,3},{8,14},{9,15},{10,12},{11,13},... | collective-permute-start | bytes 221192 | tf_op jit(solution)/shard_map/ppermute | solution.py:374
  99.5 2.0 %collective-permute-start.32 = (bf16[128,1024]{1,0:T(8,128)(2,1)S(1)}, bf16[128,1024]{1,0:T(8,128)(2,1)S(1)}, u32[]{:S(2)}, u32[]{:S(2)}) collective-permute-start(bf16[128,1024]{1,0:T(8,128)(2,1)S(1)} %get-tuple-element.73.refs_8_), channel_id=1, source_target_pairs={{0,1},{16,17}} | collective-permute-start | bytes 786440 | tf_op jit(solution)/shard_map/ppermute | solution.py:374
  101.8 1.3 %collective-permute-start.33 = (f32[8,256]{1,0:T(8,128)S(1)}, f32[8,256]{1,0:T(8,128)S(1)}, u32[]{:S(2)}, u32[]{:S(2)}) collective-permute-start(f32[8,256]{1,0:T(8,128)S(1)} %logs.1), channel_id=1, source_target_pairs={{8,0},{9,1},{10,2},{11,3},{12,4},{13,5},{14,6},{15,7},{24,16},{25,... | collective-permute-start | bytes 24584 | tf_op jit(solution)/shard_map/ppermute | solution.py:374
  103.1 14.3 %collective-permute-done.33 = f32[8,256]{1,0:T(8,128)S(1)} collective-permute-done((f32[8,256]{1,0:T(8,128)S(1)}, f32[8,256]{1,0:T(8,128)S(1)}, u32[]{:S(2)}, u32[]{:S(2)}) %collective-permute-start.33) | collective-permute-done | bytes 8224 | tf_op jit(solution)/shard_map/ppermute | solution.py:374
  118.0 1.5 %finish.1 = f32[224,2048]{1,0:T(8,128)} custom-call(bf16[32,1152]{1,0:T(8,128)(2,1)S(1)} %get-tuple-element.65.refs_0_, bf16[32,1152]{1,0:T(8,128)(2,1)S(1)} %collective-permute-done.25.refs_1_, bf16[32,1152]{1,0:T(8,128)(2,1)S(1)} %collective-permute-done.26.refs_2_, bf16[32,1152]{1,0:T(8,128)(2,1)S(1)} %collective-permute-done.27.refs_3_, ...), custom_call_target="tpu_custom_call" | custom-call | tf_op jit(solution)/shard_map/finish/pallas_call | solution.py:549
  (79 shorter events, 25.4 us)
Async XLA Ops:
  2.3 39.3 %collective-permute-start.16 = (bf16[128,2048]{1,0:T(8,128)(2,1)S(1)}, bf16[128,2048]{1,0:T(8,128)(2,1)S(1)}, u32[]{:S(2)}, u32[]{:S(2)}) collective-permute-start(bf16[128,2048]{1,0:T(8,128)(2,1)S(1)} %get-tuple-element.74), channel_id=1, source_target_pairs={{0,1},{1,0},{16,17},{17,16}} | collective-permute-start | bytes 1572872 | tf_op jit(solution)/shard_map/ppermute | solution.py:374
  5.4 5.8 %collective-permute-start.1 = (f16[72,1024]{1,0:T(8,128)(2,1)S(1)}, f16[72,1024]{1,0:T(8,128)(2,1)S(1)}, u32[]{:S(2)}, u32[]{:S(2)}) collective-permute-start(f16[72,1024]{1,0:T(8,128)(2,1)S(1)} %get-tuple-element.76), channel_id=1, source_target_pairs={{0,2},{1,3},{2,0},{3,1},{4,6},{5,7},{6,4},{7,5},{8,10},{9,11},{10,... | collective-permute-start | bytes 442376 | tf_op jit(solution)/shard_map/ppermute | solution.py:374
  6.8 36.2 %collective-permute-start.15 = (f32[64,2048]{1,0:T(8,128)S(1)}, f32[64,2048]{1,0:T(8,128)S(1)}, u32[]{:S(2)}, u32[]{:S(2)}) collective-permute-start(f32[64,2048]{1,0:T(8,128)S(1)} %bitcast.11), channel_id=1, source_target_pairs={{0,1},{1,0},{16,17},{17,16}} | collective-permute-start | bytes 1572872 | tf_op jit(solution)/shard_map/ppermute | solution.py:374
  8.7 6.8 %collective-permute-start.3 = (f16[72,1024]{1,0:T(8,128)(2,1)S(1)}, f16[72,1024]{1,0:T(8,128)(2,1)S(1)}, u32[]{:S(2)}, u32[]{:S(2)}) collective-permute-start(f16[72,1024]{1,0:T(8,128)(2,1)S(1)} %get-tuple-element.76), channel_id=1, source_target_pairs={{0,4},{1,5},{2,6},{3,7},{4,0},{5,1},{6,2},{7,3},{8,12},{9,13},{10,... | collective-permute-start | bytes 442376 | tf_op jit(solution)/shard_map/ppermute | solution.py:374
  9.1 7.2 %collective-permute-start.5 = (f16[72,1024]{1,0:T(8,128)(2,1)S(1)}, f16[72,1024]{1,0:T(8,128)(2,1)S(1)}, u32[]{:S(2)}, u32[]{:S(2)}) collective-permute-start(f16[72,1024]{1,0:T(8,128)(2,1)S(1)} %get-tuple-element.76), channel_id=1, source_target_pairs={{0,6},{1,7},{2,4},{3,5},{4,2},{5,3},{6,0},{7,1},{8,14},{9,15},{10,... | collective-permute-start | bytes 442376 | tf_op jit(solution)/shard_map/ppermute | solution.py:374
  11.3 5.1 %collective-permute-start = (f16[72,1024]{1,0:T(8,128)(2,1)S(1)}, f16[72,1024]{1,0:T(8,128)(2,1)S(1)}, u32[]{:S(2)}, u32[]{:S(2)}) collective-permute-start(f16[72,1024]{1,0:T(8,128)(2,1)S(1)} %get-tuple-element.76), channel_id=1, source_target_pairs={{0,1},{1,0},{2,3},{3,2},{4,5},{5,4},{6,7},{7,6},{8,9},{9,8},{10,11... | collective-permute-start | bytes 442376 | tf_op jit(solution)/shard_map/ppermute | solution.py:374
  30.0 27.0 %collective-permute-start.7 = (f16[72,1024]{1,0:T(8,128)(2,1)S(1)}, f16[72,1024]{1,0:T(8,128)(2,1)S(1)}, u32[]{:S(2)}, u32[]{:S(2)}) collective-permute-start(f16[72,1024]{1,0:T(8,128)(2,1)S(1)} %convert_element_type.57), channel_id=1, source_target_pairs={{0,8},{1,9},{2,10},{3,11},{4,12},{5,13},{6,14},{7,15},{16,24},{17,... | collective-permute-start | bytes 442376 | tf_op jit(solution)/shard_map/ppermute | solution.py:374
  34.3 6.1 %collective-permute-start.10 = (bf16[32,1024]{1,0:T(8,128)(2,1)S(1)}, bf16[32,1024]{1,0:T(8,128)(2,1)S(1)}, u32[]{:S(2)}, u32[]{:S(2)}) collective-permute-start(bf16[32,1024]{1,0:T(8,128)(2,1)S(1)} %get-tuple-element.45), channel_id=1, source_target_pairs={{2,1},{3,0},{5,6},{6,5},{7,4},{8,11},{9,10},{10,9},{11,8},{13,14},... | collective-permute-start | bytes 196616 | tf_op jit(solution)/shard_map/ppermute | solution.py:374
  38.9 8.2 %collective-permute-start.11 = (bf16[32,1024]{1,0:T(8,128)(2,1)S(1)}, bf16[32,1024]{1,0:T(8,128)(2,1)S(1)}, u32[]{:S(2)}, u32[]{:S(2)}) collective-permute-start(bf16[32,1024]{1,0:T(8,128)(2,1)S(1)} %get-tuple-element.46), channel_id=1, source_target_pairs={{2,6},{4,0},{5,1},{6,2},{7,3},{8,12},{9,13},{10,14},{12,8},{13,9},... | collective-permute-start | bytes 196616 | tf_op jit(solution)/shard_map/ppermute | solution.py:374
  40.4 13.3 %collective-permute-start.12 = (bf16[32,1024]{1,0:T(8,128)(2,1)S(1)}, bf16[32,1024]{1,0:T(8,128)(2,1)S(1)}, u32[]{:S(2)}, u32[]{:S(2)}) collective-permute-start(bf16[32,1024]{1,0:T(8,128)(2,1)S(1)} %get-tuple-element.47), channel_id=1, source_target_pairs={{3,6},{4,1},{5,0},{6,3},{7,2},{8,13},{9,12},{11,14},{12,9},{13,8},... | collective-permute-start | bytes 196616 | tf_op jit(solution)/shard_map/ppermute | solution.py:374
  41.7 13.3 %collective-permute-start.13 = (bf16[32,1024]{1,0:T(8,128)(2,1)S(1)}, bf16[32,1024]{1,0:T(8,128)(2,1)S(1)}, u32[]{:S(2)}, u32[]{:S(2)}) collective-permute-start(bf16[32,1024]{1,0:T(8,128)(2,1)S(1)} %get-tuple-element.48), channel_id=1, source_target_pairs={{2,4},{3,5},{4,2},{5,3},{6,0},{7,1},{8,14},{10,12},{11,13},{12,10}... | collective-permute-start | bytes 196616 | tf_op jit(solution)/shard_map/ppermute | solution.py:374
  43.0 13.3 %collective-permute-start.14 = (bf16[32,1024]{1,0:T(8,128)(2,1)S(1)}, bf16[32,1024]{1,0:T(8,128)(2,1)S(1)}, u32[]{:S(2)}, u32[]{:S(2)}) collective-permute-start(bf16[32,1024]{1,0:T(8,128)(2,1)S(1)} %get-tuple-element.49), channel_id=1, source_target_pairs={{2,5},{3,4},{4,3},{5,2},{6,1},{7,0},{9,14},{10,13},{11,12},{12,11}... | collective-permute-start | bytes 196616 | tf_op jit(solution)/shard_map/ppermute | solution.py:374
  47.1 16.1 %collective-permute-start.18 = (bf16[32,1152]{1,0:T(8,128)(2,1)S(1)}, bf16[32,1152]{1,0:T(8,128)(2,1)S(1)}, u32[]{:S(2)}, u32[]{:S(2)}) collective-permute-start(bf16[32,1152]{1,0:T(8,128)(2,1)S(1)} %get-tuple-element.51), channel_id=1, source_target_pairs={{0,2},{1,3},{16,18},{17,19}} | collective-permute-start | bytes 221192 | tf_op jit(solution)/shard_map/ppermute | solution.py:374
  53.7 9.5 %collective-permute-start.19 = (bf16[32,1152]{1,0:T(8,128)(2,1)S(1)}, bf16[32,1152]{1,0:T(8,128)(2,1)S(1)}, u32[]{:S(2)}, u32[]{:S(2)}) collective-permute-start(bf16[32,1152]{1,0:T(8,128)(2,1)S(1)} %get-tuple-element.52), channel_id=1, source_target_pairs={{0,4},{1,5},{16,20},{17,21}} | collective-permute-start | bytes 221192 | tf_op jit(solution)/shard_map/ppermute | solution.py:374
  55.0 8.2 %collective-permute-start.20 = (bf16[32,1152]{1,0:T(8,128)(2,1)S(1)}, bf16[32,1152]{1,0:T(8,128)(2,1)S(1)}, u32[]{:S(2)}, u32[]{:S(2)}) collective-permute-start(bf16[32,1152]{1,0:T(8,128)(2,1)S(1)} %get-tuple-element.53), channel_id=1, source_target_pairs={{0,6},{16,22}} | collective-permute-start | bytes 221192 | tf_op jit(solution)/shard_map/ppermute | solution.py:374
  57.0 6.2 %collective-permute-start.9 = (bf16[32,1024]{1,0:T(8,128)(2,1)S(1)}, bf16[32,1024]{1,0:T(8,128)(2,1)S(1)}, u32[]{:S(2)}, u32[]{:S(2)}) collective-permute-start(bf16[32,1024]{1,0:T(8,128)(2,1)S(1)} %get-tuple-element.44), channel_id=1, source_target_pairs={{2,0},{3,1},{4,6},{6,4},{7,5},{8,10},{9,11},{10,8},{11,9},{12,14},... | collective-permute-start | bytes 196616 | tf_op jit(solution)/shard_map/ppermute | solution.py:374
  85.6 10.3 %collective-permute-start.25 = (bf16[32,1152]{1,0:T(8,128)(2,1)S(1)}, bf16[32,1152]{1,0:T(8,128)(2,1)S(1)}, u32[]{:S(2)}, u32[]{:S(2)}) collective-permute-start(bf16[32,1152]{1,0:T(8,128)(2,1)S(1)} %get-tuple-element.66), channel_id=1, source_target_pairs={{2,3},{3,2},{4,5},{5,4},{6,7},{8,9},{9,8},{10,11},{11,10},{12,13},... | collective-permute-start | bytes 221192 | tf_op jit(solution)/shard_map/ppermute | solution.py:374
  86.3 11.9 %collective-permute-start.26 = (bf16[32,1152]{1,0:T(8,128)(2,1)S(1)}, bf16[32,1152]{1,0:T(8,128)(2,1)S(1)}, u32[]{:S(2)}, u32[]{:S(2)}) collective-permute-start(bf16[32,1152]{1,0:T(8,128)(2,1)S(1)} %get-tuple-element.67), channel_id=1, source_target_pairs={{0,2},{1,3},{4,6},{5,7},{6,4},{8,10},{9,11},{10,8},{11,9},{12,14},... | collective-permute-start | bytes 221192 | tf_op jit(solution)/shard_map/ppermute | solution.py:374
  89.9 9.6 %collective-permute-start.27 = (bf16[32,1152]{1,0:T(8,128)(2,1)S(1)}, bf16[32,1152]{1,0:T(8,128)(2,1)S(1)}, u32[]{:S(2)}, u32[]{:S(2)}) collective-permute-start(bf16[32,1152]{1,0:T(8,128)(2,1)S(1)} %get-tuple-element.68), channel_id=1, source_target_pairs={{0,3},{1,2},{4,7},{5,6},{6,5},{8,11},{9,10},{10,9},{11,8},{12,15},... | collective-permute-start | bytes 221192 | tf_op jit(solution)/shard_map/ppermute | solution.py:374
  91.2 10.4 %collective-permute-start.28 = (bf16[32,1152]{1,0:T(8,128)(2,1)S(1)}, bf16[32,1152]{1,0:T(8,128)(2,1)S(1)}, u32[]{:S(2)}, u32[]{:S(2)}) collective-permute-start(bf16[32,1152]{1,0:T(8,128)(2,1)S(1)} %get-tuple-element.69), channel_id=1, source_target_pairs={{0,4},{1,5},{2,6},{3,7},{6,2},{8,12},{9,13},{10,14},{11,15},{12,8}... | collective-permute-start | bytes 221192 | tf_op jit(solution)/shard_map/ppermute | solution.py:374
  92.5 9.1 %collective-permute-start.29 = (bf16[32,1152]{1,0:T(8,128)(2,1)S(1)}, bf16[32,1152]{1,0:T(8,128)(2,1)S(1)}, u32[]{:S(2)}, u32[]{:S(2)}) collective-permute-start(bf16[32,1152]{1,0:T(8,128)(2,1)S(1)} %get-tuple-element.70), channel_id=1, source_target_pairs={{0,5},{1,4},{2,7},{3,6},{6,3},{8,13},{9,12},{10,15},{11,14},{12,9}... | collective-permute-start | bytes 221192 | tf_op jit(solution)/shard_map/ppermute | solution.py:374
  95.9 5.7 %collective-permute-start.30 = (bf16[32,1152]{1,0:T(8,128)(2,1)S(1)}, bf16[32,1152]{1,0:T(8,128)(2,1)S(1)}, u32[]{:S(2)}, u32[]{:S(2)}) collective-permute-start(bf16[32,1152]{1,0:T(8,128)(2,1)S(1)} %get-tuple-element.71), channel_id=1, source_target_pairs={{0,6},{1,7},{2,4},{3,5},{4,2},{5,3},{8,14},{9,15},{10,12},{11,13},... | collective-permute-start | bytes 221192 | tf_op jit(solution)/shard_map/ppermute | solution.py:374
  99.5 18.5 %collective-permute-start.32 = (bf16[128,1024]{1,0:T(8,128)(2,1)S(1)}, bf16[128,1024]{1,0:T(8,128)(2,1)S(1)}, u32[]{:S(2)}, u32[]{:S(2)}) collective-permute-start(bf16[128,1024]{1,0:T(8,128)(2,1)S(1)} %get-tuple-element.73.refs_8_), channel_id=1, source_target_pairs={{0,1},{16,17}} | collective-permute-start | bytes 786440 | tf_op jit(solution)/shard_map/ppermute | solution.py:374
  101.8 15.6 %collective-permute-start.33 = (f32[8,256]{1,0:T(8,128)S(1)}, f32[8,256]{1,0:T(8,128)S(1)}, u32[]{:S(2)}, u32[]{:S(2)}) collective-permute-start(f32[8,256]{1,0:T(8,128)S(1)} %logs.1), channel_id=1, source_target_pairs={{8,0},{9,1},{10,2},{11,3},{12,4},{13,5},{14,6},{15,7},{24,16},{25,... | collective-permute-start | bytes 24584 | tf_op jit(solution)/shard_map/ppermute | solution.py:374
  (15 other events, 59.8 us)

commit v2 on v1

--- a/solution.py
+++ b/solution.py
@@ -7,6 +7,7 @@
 from jax.experimental import pallas as pl
 from jax.experimental.pallas import tpu as pltpu
 from jax.sharding import PartitionSpec as P
+
 
 A_DECAY = 0.8
 EPS_SCALE = 0.05
@@ -25,6 +26,10 @@
 def params(mib, grid=False):
     semantics = ("arbitrary",) if grid else None
     return pltpu.CompilerParams(vmem_limit_bytes=mib << 20, dimension_semantics=semantics)
+
+
+def launch(body, **spec):
+    return pl.pallas_call(body, **spec)
 
 
 def block_of(device):
@@ -140,8 +145,8 @@
 
 def build(last_position, *refs):
     slots, tail_ref = refs[:TEAM], refs[TEAM]
-    kernel_ref, seventh_ref, sup_ref, sums_ref = refs[TEAM + 1 : TEAM + 5]
-    points, turned, features = refs[TEAM + 5 :]
+    kernel_ref, opening_ref, seventh_ref, sup_ref, sums_ref = refs[TEAM + 1 : TEAM + 6]
+    points, turned, features = refs[TEAM + 6 :]
     position = lax.axis_index("tm")
     device, team = position % TEAM, position // TEAM
     last_team = last_position // TEAM
@@ -154,6 +159,7 @@
             points[device ^ mask] = slot[...]
         for index in range(TEAM):
             sup_ref[index : index + 1, :] = points[index, dims : dims + 1, :LOGS]
+        opening_ref[...] = points[0]
         seventh_ref[...] = points[TEAM - 1]
         sums_ref[...] = jnp.zeros_like(sums_ref)
 
@@ -373,41 +379,39 @@
     def move(value, pairs):
         return lax.ppermute(value, "tm", pairs)
 
-    def swap(value, mask, keep=lambda source, target: True):
-        pairs = [(i, i ^ mask) for i in range(devices) if keep(i, i ^ mask)]
-        return move(value, pairs)
-
-    other_points = move(points, [(0, 1), (1, 0)])
-    first_support = move(supports, [(1, 0)])
+    def swap(value, mask):
+        return move(value, [(i, i ^ mask) for i in range(devices)])
+
+    def shifted(value, steps):
+        return move(value, [(i, (i + steps) % devices) for i in range(devices)])
+
+    other_points = swap(points, 1)
+    first_support = swap(supports, 1)
     half = 4 * BLOCK
     padded = jnp.pad(potentials, ((0, 2 * half - columns), (0, 0)), constant_values=1.0)
     mine = jnp.where(position == 1, half, 0)
     own_pots = lax.dynamic_slice_in_dim(padded, mine, half, 0).astype(BF16)
     sent_pots = lax.dynamic_slice_in_dim(padded, half - mine, half, 0).astype(BF16)
-    other_pots = move(sent_pots, [(0, 1), (1, 0)])
+    other_pots = swap(sent_pots, 1)
 
     payload = jnp.concatenate(
         [points[:, :LIVE], jnp.broadcast_to(supports.astype(F32), (SUP, LIVE))], axis=0
     ).astype(jnp.float16)
     far = [payload] + [swap(payload, mask) for mask in (2, 4, 6)]
 
-    pots = pl.pallas_call(
+    pots = launch(
         split_pots,
         grid=(1,),
         out_shape=[shape(BLOCK, LIVE)] * TEAM,
         in_specs=[pl.BlockSpec((columns, LIVE), lambda i: (0, 0))],
         out_specs=[pl.BlockSpec((BLOCK, LIVE), lambda i: (0, 0))] * TEAM,
         compiler_params=params(16),
-        name="pots",
     )(potentials)
 
-    def holds(source, target):
-        return 2 <= source < last and target % TEAM != TEAM - 1
-
-    pots = [pots[0]] + [swap(pots[mask], mask, holds) for mask in range(1, TEAM)]
+    pots = [pots[0]] + [swap(pots[mask], mask) for mask in range(1, TEAM)]
 
     support_one = jnp.where(position == 1, supports, first_support).astype(F32)
-    *opened, early = pl.pallas_call(
+    *opened, early = launch(
         first_step,
         out_shape=[shape(BLOCK, LIVE + LOGS)] * 4 + [shape(half, LIVE)],
         in_specs=[VMEM, VMEM, VMEM, VMEM, smem],
@@ -422,13 +426,11 @@
             scratch(count, LIVE),
         ],
         compiler_params=params(24),
-        name="first",
     )(points, other_points, own_pots, other_pots, support_one)
-    early_other = move(early, [(0, 1)])
+    early_other = swap(early, 1)
     arrived = [opened[0]]
     for index in range(1, 4):
-        pairs = [(c, c + 2 * index) for c in range(2) if c + 2 * index < TEAM - 1]
-        arrived.append(move(opened[index], pairs))
+        arrived.append(swap(opened[index], 2 * index))
 
     near = [swap(value, 1) for value in far]
     slots = [None] * TEAM
@@ -437,11 +439,12 @@
         slots[mask + 1] = near[index].astype(F32)
 
     full = pl.BlockSpec((dims + SUP, LIVE), lambda i: (0, 0))
-    kernels, seventh, team_sup, sums = pl.pallas_call(
+    kernels, opening, seventh, team_sup, sums = launch(
         functools.partial(build, last),
         grid=(TEAM + 1,),
         out_shape=[
-            shape(TEAM + 1, LIVE, LIVE),
+            pltpu.HBM((TEAM + 1, LIVE, LIVE), BF16),
+            shape(dims + SUP, LIVE, dtype=F32),
             shape(dims + SUP, LIVE, dtype=F32),
             shape(TEAM, LOGS, dtype=F32),
             shape(8, LIVE, dtype=F32),
@@ -449,6 +452,7 @@
         in_specs=[full] * TEAM + [pl.BlockSpec((dims, LIVE), lambda i: (0, 1))],
         out_specs=[
             pl.BlockSpec((1, LIVE, LIVE), lambda i: (i, 0, 0)),
+            full,
             full,
             pl.BlockSpec((TEAM, LOGS), lambda i: (0, 0)),
             pl.BlockSpec((8, LIVE), lambda i: (0, 0)),
@@ -459,8 +463,9 @@
             scratch(depth, LIVE),
         ],
         compiler_params=params(24, True),
-        name="build",
     )(*slots, points)
+
+    kernels = pltpu.with_memory_space_constraint(kernels, pltpu.HBM)
 
     def run_sweep(stage, opening, sums, incoming, previous):
         flag = (position // TEAM == stage).astype(jnp.int32).reshape(1)
@@ -473,7 +478,7 @@
             return pl.BlockSpec(dims, lambda i, flag: (0,) * len(dims))
 
         wide = whole(BLOCK, LIVE + LOGS)
-        return pl.pallas_call(
+        return launch(
             functools.partial(sweep, stage, teams - 1, previous is not None, len(incoming)),
             grid_spec=pltpu.PrefetchScalarGridSpec(
                 num_scalar_prefetch=1,
@@ -497,12 +502,9 @@
             ),
             out_shape=[shape(BLOCK, LIVE + LOGS)] * (TEAM + 1),
             compiler_params=params(24, True),
-            name="sweep%d" % min(stage, 1),
         )(flag, kernels, opening, team_sup, sums, *pots, *incoming, *(previous or []))
 
-    before = move(
-        seventh.astype(jnp.float16), [(i, i + TEAM) for i in range(devices - TEAM)]
-    ).astype(F32)
+    before = shifted(seventh.astype(jnp.float16), TEAM).astype(F32)
     *blocks, leaving = run_sweep(0, sums, sums, arrived, None)
 
     for stage in range(1, teams):
@@ -510,27 +512,21 @@
         incoming = move(leaving, [(base - TEAM + i, base + i) for i in range(TEAM - 1)])
         if stage == 1:
             before, sums, leaving = lax.optimization_barrier((before, sums, leaving))
-            opening = pl.pallas_call(
+            opening = launch(
                 bridge,
                 out_shape=shape(LIVE, LIVE),
                 in_specs=[VMEM, VMEM],
                 out_specs=VMEM,
                 scratch_shapes=[scratch(LIVE, depth), scratch(depth, LIVE)],
                 compiler_params=params(16),
-                name="bridge",
-            )(before, start_of(slots, position))
-            top = devices - TEAM
+            )(before, opening)
             for mask in (4, 2, 1):
-                sources = [i for i in range(TEAM) if i % (2 * mask) == 2 * mask - 1]
-                sums = sums + move(sums, [(top + i, top + i - mask) for i in sources])
+                sums = sums + swap(sums, mask)
         *blocks, leaving = run_sweep(stage, opening, sums, [incoming], blocks)
 
-    def ready(source, target):
-        return source % TEAM != TEAM - 1 and target > 1
-
-    blocks = [blocks[0]] + [swap(blocks[mask], mask, ready) for mask in range(1, TEAM)]
+    blocks = [blocks[0]] + [swap(blocks[mask], mask) for mask in range(1, TEAM)]
     lanes = pl.BlockSpec((BLOCK, LOGS), lambda i: (0, LIVE // LOGS))
-    logs = pl.pallas_call(
+    logs = launch(
         functools.partial(gather_logs, 1.0 / last),
         grid=(1,),
         out_shape=shape(8, TEAM * BLOCK, dtype=F32),
@@ -538,15 +534,14 @@
         out_specs=pl.BlockSpec((8, TEAM * BLOCK), lambda i: (0, 0)),
         scratch_shapes=[scratch(TEAM * BLOCK, LOGS, dtype=F32)],
         compiler_params=params(16),
-        name="logs",
     )(*blocks)
     for team in range(teams - 1):
         shift = (teams - 1 - team) * TEAM
-        moved = move(logs, [(devices - TEAM + i, devices - TEAM + i - shift) for i in range(TEAM)])
+        moved = shifted(logs, -shift)
         logs = jnp.where(position // TEAM == team, moved, logs)
     log_scale = logs[0, :columns]
 
-    messages = pl.pallas_call(
+    messages = launch(
         functools.partial(finish, last),
         out_shape=shape(columns, count, dtype=F32),
         in_specs=[VMEM] * (TEAM + 2) + [smem, anywhere],
@@ -557,17 +552,8 @@
             pltpu.SemaphoreType.DMA((2,)),
         ],
         compiler_params=params(24),
-        name="finish",
     )(*blocks, early, early_other, supports, kernels)
     return messages[None], log_scale
-
-
-def start_of(slots, position):
-    device = position % TEAM
-    value = slots[0]
-    for mask in range(1, TEAM):
-        value = jnp.where(device == mask, slots[mask], value)
-    return value
 
 
 def solution(mesh):

time: 121 us -> 93.2 us (0.77)
  local copies, waits for them, and re-layouts: 20.8 us -> 1.66 us
  starting transfers between devices: 50.6 us -> 35.3 us
  Pallas kernels: 14.6 us -> 24.8 us
  waiting for transfers between devices: 29.9 us -> 27.4 us
    unnamed x10 -> x4, local copies, waits for them, and re-layouts: 19.2 us -> 0.01 us
    ppermute x34, starting transfers between devices: 50.6 us -> 35.3 us  [move(): return lax.ppermute(value, 'tm', pairs)]
    pallas_call x8, Pallas kernels: 14.6 us -> 24.8 us  [the longest x2 11 us: run_sweep(): launch(functools.partial(sweep, stage, teams - 1, previous is not None, l...]
    ppermute x34, waiting for transfers between devices: 29.9 us -> 27.4 us  [move(): return lax.ppermute(value, 'tm', pairs)]
  transfers between devices with their start and end apart: 34 -> 34, of which waited for: 10 -> 18; matrix products, arithmetic and copies ran while one was open for 1% -> 1% of each run, Pallas kernels for 7% -> 13%
where the time goes in v2:
time: 93.2 us; the launch traced here: 92.1 us
  starting transfers between devices  35.3 us (38%)
  waiting for transfers between devices  27.4 us (29%)
  Pallas kernels  24.8 us (27%)
  between operations  2.21 us (2%)
  local copies, waits for them, and re-layouts  1.66 us (2%)
    ppermute x34, starting transfers between devices, move(): return lax.ppermute(value, 'tm', pairs)  35.3 us
    ppermute x34, waiting for transfers between devices, move(): return lax.ppermute(value, 'tm', pairs)  27.4 us
    pallas_call x2, Pallas kernels, run_sweep(): launch(functools.partial(sweep, stage, teams - 1, previous is not None, l...  11 us
    pallas_call x1, Pallas kernels, per_device(): launch(functools.partial(build, last), grid=(TEAM + 1,), out_shape=[pltpu...  9.84 us
    pallas_call x1, Pallas kernels, per_device(): launch(first_step, out_shape=[shape(BLOCK, LIVE + LOGS)] * 4 + [shape(hal...  2.17 us
  transfers between devices with their start and end apart: 34, of which 18 were waited for; matrix products, arithmetic and copies ran while one was open for 1% of the time, Pallas kernels for 13%

profile of v2, /device:TPU:0, one launch (start us, length us, event | category | flops | bytes accessed | tf_op | source)
XLA Modules:
  0.0 92.1 jit_solution(2625982991971409037)
XLA Ops:
  0.6 1.6 %fusion.1 = (bf16[128,2048]{1,0:T(8,128)(2,1)S(1)}, bf16[128,2048]{1,0:T(8,128)(2,1)S(1)}) fusion(s32[]{:T(128)S(6)} %select_n.33, f32[224,2048]{1,0:T(8,128)} %bitcast.8, s32[]{:T(128)S(6)} %select_n.32), kind=kLoop, calls=%fused_computation.3 | loop fusion | bytes 2883592 | tf_op jit(solution)/shard_map/convert_element_type | solution.py:394
  3.6 2.6 %collective-permute-start.1 = (f16[72,1024]{1,0:T(8,128)(2,1)S(1)}, f16[72,1024]{1,0:T(8,128)(2,1)S(1)}, u32[]{:S(2)}, u32[]{:S(2)}) collective-permute-start(f16[72,1024]{1,0:T(8,128)(2,1)S(1)} %get-tuple-element.78), channel_id=1, source_target_pairs={{0,2},{1,3},{2,0},{3,1},{4,6},{5,7},{6,4},{7,5},{8,10},{9,11},{10,... | collective-permute-start | bytes 442376 | tf_op jit(solution)/shard_map/ppermute | solution.py:380
  6.4 1.6 %collective-permute-start.3 = (f16[72,1024]{1,0:T(8,128)(2,1)S(1)}, f16[72,1024]{1,0:T(8,128)(2,1)S(1)}, u32[]{:S(2)}, u32[]{:S(2)}) collective-permute-start(f16[72,1024]{1,0:T(8,128)(2,1)S(1)} %get-tuple-element.78), channel_id=1, source_target_pairs={{0,4},{1,5},{2,6},{3,7},{4,0},{5,1},{6,2},{7,3},{8,12},{9,13},{10,... | collective-permute-start | bytes 442376 | tf_op jit(solution)/shard_map/ppermute | solution.py:380
  8.2 2.5 %collective-permute-done.1 = f16[72,1024]{1,0:T(8,128)(2,1)S(1)} collective-permute-done((f16[72,1024]{1,0:T(8,128)(2,1)S(1)}, f16[72,1024]{1,0:T(8,128)(2,1)S(1)}, u32[]{:S(2)}, u32[]{:S(2)}) %collective-permute-start.1) | collective-permute-done | bytes 147488 | tf_op jit(solution)/shard_map/ppermute | solution.py:380
  10.7 2.4 %collective-permute-done.3 = f16[72,1024]{1,0:T(8,128)(2,1)S(1)} collective-permute-done((f16[72,1024]{1,0:T(8,128)(2,1)S(1)}, f16[72,1024]{1,0:T(8,128)(2,1)S(1)}, u32[]{:S(2)}, u32[]{:S(2)}) %collective-permute-start.3) | collective-permute-done | bytes 147488 | tf_op jit(solution)/shard_map/ppermute | solution.py:380
  13.1 2.3 %collective-permute-done.5 = f16[72,1024]{1,0:T(8,128)(2,1)S(1)} collective-permute-done((f16[72,1024]{1,0:T(8,128)(2,1)S(1)}, f16[72,1024]{1,0:T(8,128)(2,1)S(1)}, u32[]{:S(2)}, u32[]{:S(2)}) %collective-permute-start.5) | collective-permute-done | bytes 147488 | tf_op jit(solution)/shard_map/ppermute | solution.py:380
  17.0 9.8 %shard_map.50 = (bf16[9,1024,1024]{2,1,0:T(8,128)(2,1)}, f32[72,1024]{1,0:T(8,128)S(1)}, f32[72,1024]{1,0:T(8,128)S(1)}, f32[8,128]{1,0:T(8,128)S(1)}, f32[8,1024]{1,0:T(8,128)S(1)}) custom-call(f32[72,1024]{1,0:T(8,128)S(1)} %get-tuple-element.79.refs_0_, f32[72,1024]{1,0:T(8,128)S(1)} %convert_element_type.50.refs_1_, ...), custom_call_target="tpu_custom_call" | custom-call | tf_op jit(solution)/shard_map/pallas_call | solution.py:442
  26.8 2.5 %collective-permute-start.7 = (f16[72,1024]{1,0:T(8,128)(2,1)S(1)}, f16[72,1024]{1,0:T(8,128)(2,1)S(1)}, u32[]{:S(2)}, u32[]{:S(2)}) collective-permute-start(f16[72,1024]{1,0:T(8,128)(2,1)S(1)} %convert_element_type.57), channel_id=1, source_target_pairs={{0,8},{1,9},{2,10},{3,11},{4,12},{5,13},{6,14},{7,15},{8,0},{9,1},... | collective-permute-start | bytes 442376 | tf_op jit(solution)/shard_map/ppermute | solution.py:380
  32.2 3.2 %collective-permute-start.11 = (bf16[32,1024]{1,0:T(8,128)(2,1)S(1)}, bf16[32,1024]{1,0:T(8,128)(2,1)S(1)}, u32[]{:S(2)}, u32[]{:S(2)}) collective-permute-start(bf16[32,1024]{1,0:T(8,128)(2,1)S(1)} %get-tuple-element.47), channel_id=1, source_target_pairs={{0,4},{1,5},{2,6},{3,7},{4,0},{5,1},{6,2},{7,3},{8,12},{9,13},{10,... | collective-permute-start | bytes 196616 | tf_op jit(solution)/shard_map/ppermute | solution.py:380
  35.4 1.3 %collective-permute-start.13 = (bf16[32,1024]{1,0:T(8,128)(2,1)S(1)}, bf16[32,1024]{1,0:T(8,128)(2,1)S(1)}, u32[]{:S(2)}, u32[]{:S(2)}) collective-permute-start(bf16[32,1024]{1,0:T(8,128)(2,1)S(1)} %get-tuple-element.49), channel_id=1, source_target_pairs={{0,6},{1,7},{2,4},{3,5},{4,2},{5,3},{6,0},{7,1},{8,14},{9,15},{10,... | collective-permute-start | bytes 196616 | tf_op jit(solution)/shard_map/ppermute | solution.py:380
  36.7 1.7 %collective-permute-start.14 = (bf16[32,1024]{1,0:T(8,128)(2,1)S(1)}, bf16[32,1024]{1,0:T(8,128)(2,1)S(1)}, u32[]{:S(2)}, u32[]{:S(2)}) collective-permute-start(bf16[32,1024]{1,0:T(8,128)(2,1)S(1)} %get-tuple-element.50), channel_id=1, source_target_pairs={{0,7},{1,6},{2,5},{3,4},{4,3},{5,2},{6,1},{7,0},{8,15},{9,14},{10,... | collective-permute-start | bytes 196616 | tf_op jit(solution)/shard_map/ppermute | solution.py:380
  39.1 2.2 %shard_map.52 = (bf16[32,1152]{1,0:T(8,128)(2,1)S(1)}, bf16[32,1152]{1,0:T(8,128)(2,1)S(1)}, bf16[32,1152]{1,0:T(8,128)(2,1)S(1)}, bf16[32,1152]{1,0:T(8,128)(2,1)S(1)}, bf16[128,1024]{1,0:T(8,128)(2,1)S(1)}) custom-call(f32[64,2048]{1,0:T(8,128)S(1)} %bitcast.13, f32[64,2048]{1,0:T(8,128)S(1)} %collective-permute-done.15.other_ref, ...), custom_call_target="tpu_custom_call" | custom-call | tf_op jit(solution)/shard_map/pallas_call | solution.py:414
  42.0 2.8 %collective-permute-start.20 = (bf16[32,1152]{1,0:T(8,128)(2,1)S(1)}, bf16[32,1152]{1,0:T(8,128)(2,1)S(1)}, u32[]{:S(2)}, u32[]{:S(2)}) collective-permute-start(bf16[32,1152]{1,0:T(8,128)(2,1)S(1)} %get-tuple-element.54), channel_id=1, source_target_pairs={{0,6},{1,7},{2,4},{3,5},{4,2},{5,3},{6,0},{7,1},{8,14},{9,15},{10,... | collective-permute-start | bytes 221192 | tf_op jit(solution)/shard_map/ppermute | solution.py:380
  46.1 3.7 %collective-permute-done.9.refs_6_ = bf16[32,1024]{1,0:T(8,128)(2,1)S(1)} collective-permute-done((bf16[32,1024]{1,0:T(8,128)(2,1)S(1)}, bf16[32,1024]{1,0:T(8,128)(2,1)S(1)}, u32[]{:S(2)}, u32[]{:S(2)}) %collective-permute-start.9) | collective-permute-done | bytes 65568 | tf_op jit(solution)/shard_map/ppermute | solution.py:380
  49.8 8.7 %shard_map.53 = (bf16[32,1152]{1,0:T(8,128)(2,1)S(1)}, bf16[32,1152]{1,0:T(8,128)(2,1)S(1)}, bf16[32,1152]{1,0:T(8,128)(2,1)S(1)}, bf16[32,1152]{1,0:T(8,128)(2,...) custom-call(s32[1]{0:T(128)} %bitcast.3.flag_ref, ...), custom_call_target="tpu_custom_call" | custom-call | tf_op jit(solution)/shard_map/pallas_call | solution.py:481
  59.0 1.3 %collective-permute-start.24 = (bf16[32,1152]{1,0:T(8,128)(2,1)S(1)}, bf16[32,1152]{1,0:T(8,128)(2,1)S(1)}, u32[]{:S(2)}, u32[]{:S(2)}) collective-permute-start(bf16[32,1152]{1,0:T(8,128)(2,1)S(1)} %get-tuple-element.55), channel_id=1, source_target_pairs={{0,8},{1,9},{2,10},{3,11},{4,12},{5,13},{6,14},{16,24},{17,25},{18... | collective-permute-start | bytes 221192 | tf_op jit(solution)/shard_map/ppermute | solution.py:380
  60.2 2.2 %collective-permute-done.21 = f32[8,1024]{1,0:T(8,128)S(1)} collective-permute-done((f32[8,1024]{1,0:T(8,128)S(1)}, f32[8,1024]{1,0:T(8,128)S(1)}, u32[]{:S(2)}, u32[]{:S(2)}) %collective-permute-start.21) | collective-permute-done | bytes 32800 | tf_op jit(solution)/shard_map/ppermute | solution.py:380
  63.0 3.4 %collective-permute-done.22 = f32[8,1024]{1,0:T(8,128)S(1)} collective-permute-done((f32[8,1024]{1,0:T(8,128)S(1)}, f32[8,1024]{1,0:T(8,128)S(1)}, u32[]{:S(2)}, u32[]{:S(2)}) %collective-permute-start.22) | collective-permute-done | bytes 32800 | tf_op jit(solution)/shard_map/ppermute | solution.py:380
  67.6 2.3 %shard_map.55 = (bf16[32,1152]{1,0:T(8,128)(2,1)S(1)}, bf16[32,1152]{1,0:T(8,128)(2,1)S(1)}, bf16[32,1152]{1,0:T(8,128)(2,1)S(1)}, bf16[32,1152]{1,0:T(8,128)(2,...) custom-call(s32[1]{0:T(128)} %bitcast.flag_ref, ...), custom_call_target="tpu_custom_call" | custom-call | tf_op jit(solution)/shard_map/pallas_call | solution.py:481
  72.2 1.4 %collective-permute-start.29 = (bf16[32,1152]{1,0:T(8,128)(2,1)S(1)}, bf16[32,1152]{1,0:T(8,128)(2,1)S(1)}, u32[]{:S(2)}, u32[]{:S(2)}) collective-permute-start(bf16[32,1152]{1,0:T(8,128)(2,1)S(1)} %get-tuple-element.72), channel_id=1, source_target_pairs={{0,5},{1,4},{2,7},{3,6},{4,1},{5,0},{6,3},{7,2},{8,13},{9,12},{10,... | collective-permute-start | bytes 221192 | tf_op jit(solution)/shard_map/ppermute | solution.py:380
  77.5 2.5 %collective-permute-done.30.refs_6_ = bf16[32,1152]{1,0:T(8,128)(2,1)S(1)} collective-permute-done((bf16[32,1152]{1,0:T(8,128)(2,1)S(1)}, bf16[32,1152]{1,0:T(8,128)(2,1)S(1)}, u32[]{:S(2)}, u32[]{:S(2)}) %collective-permute-start.30) | collective-permute-done | bytes 73760 | tf_op jit(solution)/shard_map/ppermute | solution.py:380
  80.9 7.6 %collective-permute-start.33 = (f32[8,256]{1,0:T(8,128)S(1)}, f32[8,256]{1,0:T(8,128)S(1)}, u32[]{:S(2)}, u32[]{:S(2)}) collective-permute-start(f32[8,256]{1,0:T(8,128)S(1)} %shard_map.57), channel_id=1, source_target_pairs={{0,8},{1,9},{2,10},{3,11},{4,12},{5,13},{6,14},{7,15},{8,0},{9,1},... | collective-permute-start | bytes 24584 | tf_op jit(solution)/shard_map/ppermute | solution.py:380
  88.4 1.6 %collective-permute-done.33 = f32[8,256]{1,0:T(8,128)S(1)} collective-permute-done((f32[8,256]{1,0:T(8,128)S(1)}, f32[8,256]{1,0:T(8,128)S(1)}, u32[]{:S(2)}, u32[]{:S(2)}) %collective-permute-start.33) | collective-permute-done | bytes 8224 | tf_op jit(solution)/shard_map/ppermute | solution.py:380
  90.6 1.5 %shard_map.56 = f32[224,2048]{1,0:T(8,128)} custom-call(bf16[32,1152]{1,0:T(8,128)(2,1)S(1)} %get-tuple-element.67.refs_0_, bf16[32,1152]{1,0:T(8,128)(2,1)S(1)} %collective-permute-done.25.refs_1_, bf16[32,1152]{1,0:T(8,128)(2,1)S(1)} %collective-permute-done.26.refs_2_, bf16[32,1152]{1,0:T(8,128)(2,1)S(1)} %collective-permute-done.27.refs_3_, ...), custom_call_target="tpu_custom_call" | custom-call | tf_op jit(solution)/shard_map/pallas_call | solution.py:544
  (72 shorter events, 17.2 us)
Async XLA Ops:
  2.3 33.1 %collective-permute-start.16 = (bf16[128,2048]{1,0:T(8,128)(2,1)S(1)}, bf16[128,2048]{1,0:T(8,128)(2,1)S(1)}, u32[]{:S(2)}, u32[]{:S(2)}) collective-permute-start(bf16[128,2048]{1,0:T(8,128)(2,1)S(1)} %get-tuple-element.76), channel_id=1, source_target_pairs={{0,1},{1,0},{2,3},{3,2},{4,5},{5,4},{6,7},{7,6},{8,9},{9,8},{10,11... | collective-permute-start | bytes 1572872 | tf_op jit(solution)/shard_map/ppermute | solution.py:380
  3.6 7.1 %collective-permute-start.1 = (f16[72,1024]{1,0:T(8,128)(2,1)S(1)}, f16[72,1024]{1,0:T(8,128)(2,1)S(1)}, u32[]{:S(2)}, u32[]{:S(2)}) collective-permute-start(f16[72,1024]{1,0:T(8,128)(2,1)S(1)} %get-tuple-element.78), channel_id=1, source_target_pairs={{0,2},{1,3},{2,0},{3,1},{4,6},{5,7},{6,4},{7,5},{8,10},{9,11},{10,... | collective-permute-start | bytes 442376 | tf_op jit(solution)/shard_map/ppermute | solution.py:380
  6.2 30.5 %collective-permute-start.15 = (f32[64,2048]{1,0:T(8,128)S(1)}, f32[64,2048]{1,0:T(8,128)S(1)}, u32[]{:S(2)}, u32[]{:S(2)}) collective-permute-start(f32[64,2048]{1,0:T(8,128)S(1)} %bitcast.11), channel_id=1, source_target_pairs={{0,1},{1,0},{2,3},{3,2},{4,5},{5,4},{6,7},{7,6},{8,9},{9,8},{10,11... | collective-permute-start | bytes 1572872 | tf_op jit(solution)/shard_map/ppermute | solution.py:380
  6.4 6.7 %collective-permute-start.3 = (f16[72,1024]{1,0:T(8,128)(2,1)S(1)}, f16[72,1024]{1,0:T(8,128)(2,1)S(1)}, u32[]{:S(2)}, u32[]{:S(2)}) collective-permute-start(f16[72,1024]{1,0:T(8,128)(2,1)S(1)} %get-tuple-element.78), channel_id=1, source_target_pairs={{0,4},{1,5},{2,6},{3,7},{4,0},{5,1},{6,2},{7,3},{8,12},{9,13},{10,... | collective-permute-start | bytes 442376 | tf_op jit(solution)/shard_map/ppermute | solution.py:380
  8.0 7.4 %collective-permute-start.5 = (f16[72,1024]{1,0:T(8,128)(2,1)S(1)}, f16[72,1024]{1,0:T(8,128)(2,1)S(1)}, u32[]{:S(2)}, u32[]{:S(2)}) collective-permute-start(f16[72,1024]{1,0:T(8,128)(2,1)S(1)} %get-tuple-element.78), channel_id=1, source_target_pairs={{0,6},{1,7},{2,4},{3,5},{4,2},{5,3},{6,0},{7,1},{8,14},{9,15},{10,... | collective-permute-start | bytes 442376 | tf_op jit(solution)/shard_map/ppermute | solution.py:380
  26.8 18.0 %collective-permute-start.7 = (f16[72,1024]{1,0:T(8,128)(2,1)S(1)}, f16[72,1024]{1,0:T(8,128)(2,1)S(1)}, u32[]{:S(2)}, u32[]{:S(2)}) collective-permute-start(f16[72,1024]{1,0:T(8,128)(2,1)S(1)} %convert_element_type.57), channel_id=1, source_target_pairs={{0,8},{1,9},{2,10},{3,11},{4,12},{5,13},{6,14},{7,15},{8,0},{9,1},... | collective-permute-start | bytes 442376 | tf_op jit(solution)/shard_map/ppermute | solution.py:380
  29.5 5.9 %collective-permute-start.10 = (bf16[32,1024]{1,0:T(8,128)(2,1)S(1)}, bf16[32,1024]{1,0:T(8,128)(2,1)S(1)}, u32[]{:S(2)}, u32[]{:S(2)}) collective-permute-start(bf16[32,1024]{1,0:T(8,128)(2,1)S(1)} %get-tuple-element.46), channel_id=1, source_target_pairs={{0,3},{1,2},{2,1},{3,0},{4,7},{5,6},{6,5},{7,4},{8,11},{9,10},{10,... | collective-permute-start | bytes 196616 | tf_op jit(solution)/shard_map/ppermute | solution.py:380
  32.2 9.1 %collective-permute-start.11 = (bf16[32,1024]{1,0:T(8,128)(2,1)S(1)}, bf16[32,1024]{1,0:T(8,128)(2,1)S(1)}, u32[]{:S(2)}, u32[]{:S(2)}) collective-permute-start(bf16[32,1024]{1,0:T(8,128)(2,1)S(1)} %get-tuple-element.47), channel_id=1, source_target_pairs={{0,4},{1,5},{2,6},{3,7},{4,0},{5,1},{6,2},{7,3},{8,12},{9,13},{10,... | collective-permute-start | bytes 196616 | tf_op jit(solution)/shard_map/ppermute | solution.py:380
  35.4 6.0 %collective-permute-start.12 = (bf16[32,1024]{1,0:T(8,128)(2,1)S(1)}, bf16[32,1024]{1,0:T(8,128)(2,1)S(1)}, u32[]{:S(2)}, u32[]{:S(2)}) collective-permute-start(bf16[32,1024]{1,0:T(8,128)(2,1)S(1)} %get-tuple-element.48), channel_id=1, source_target_pairs={{0,5},{1,4},{2,7},{3,6},{4,1},{5,0},{6,3},{7,2},{8,13},{9,12},{10,... | collective-permute-start | bytes 196616 | tf_op jit(solution)/shard_map/ppermute | solution.py:380
  35.4 6.6 %collective-permute-start.13 = (bf16[32,1024]{1,0:T(8,128)(2,1)S(1)}, bf16[32,1024]{1,0:T(8,128)(2,1)S(1)}, u32[]{:S(2)}, u32[]{:S(2)}) collective-permute-start(bf16[32,1024]{1,0:T(8,128)(2,1)S(1)} %get-tuple-element.49), channel_id=1, source_target_pairs={{0,6},{1,7},{2,4},{3,5},{4,2},{5,3},{6,0},{7,1},{8,14},{9,15},{10,... | collective-permute-start | bytes 196616 | tf_op jit(solution)/shard_map/ppermute | solution.py:380
  36.7 8.2 %collective-permute-start.14 = (bf16[32,1024]{1,0:T(8,128)(2,1)S(1)}, bf16[32,1024]{1,0:T(8,128)(2,1)S(1)}, u32[]{:S(2)}, u32[]{:S(2)}) collective-permute-start(bf16[32,1024]{1,0:T(8,128)(2,1)S(1)} %get-tuple-element.50), channel_id=1, source_target_pairs={{0,7},{1,6},{2,5},{3,4},{4,3},{5,2},{6,1},{7,0},{8,15},{9,14},{10,... | collective-permute-start | bytes 196616 | tf_op jit(solution)/shard_map/ppermute | solution.py:380
  41.3 8.5 %collective-permute-start.18 = (bf16[32,1152]{1,0:T(8,128)(2,1)S(1)}, bf16[32,1152]{1,0:T(8,128)(2,1)S(1)}, u32[]{:S(2)}, u32[]{:S(2)}) collective-permute-start(bf16[32,1152]{1,0:T(8,128)(2,1)S(1)} %get-tuple-element.52), channel_id=1, source_target_pairs={{0,2},{1,3},{2,0},{3,1},{4,6},{5,7},{6,4},{7,5},{8,10},{9,11},{10,... | collective-permute-start | bytes 221192 | tf_op jit(solution)/shard_map/ppermute | solution.py:380
  41.4 8.4 %collective-permute-start.19 = (bf16[32,1152]{1,0:T(8,128)(2,1)S(1)}, bf16[32,1152]{1,0:T(8,128)(2,1)S(1)}, u32[]{:S(2)}, u32[]{:S(2)}) collective-permute-start(bf16[32,1152]{1,0:T(8,128)(2,1)S(1)} %get-tuple-element.53), channel_id=1, source_target_pairs={{0,4},{1,5},{2,6},{3,7},{4,0},{5,1},{6,2},{7,3},{8,12},{9,13},{10,... | collective-permute-start | bytes 221192 | tf_op jit(solution)/shard_map/ppermute | solution.py:380
  42.0 7.8 %collective-permute-start.20 = (bf16[32,1152]{1,0:T(8,128)(2,1)S(1)}, bf16[32,1152]{1,0:T(8,128)(2,1)S(1)}, u32[]{:S(2)}, u32[]{:S(2)}) collective-permute-start(bf16[32,1152]{1,0:T(8,128)(2,1)S(1)} %get-tuple-element.54), channel_id=1, source_target_pairs={{0,6},{1,7},{2,4},{3,5},{4,2},{5,3},{6,0},{7,1},{8,14},{9,15},{10,... | collective-permute-start | bytes 221192 | tf_op jit(solution)/shard_map/ppermute | solution.py:380
  44.9 4.9 %collective-permute-start.9 = (bf16[32,1024]{1,0:T(8,128)(2,1)S(1)}, bf16[32,1024]{1,0:T(8,128)(2,1)S(1)}, u32[]{:S(2)}, u32[]{:S(2)}) collective-permute-start(bf16[32,1024]{1,0:T(8,128)(2,1)S(1)} %get-tuple-element.45), channel_id=1, source_target_pairs={{0,2},{1,3},{2,0},{3,1},{4,6},{5,7},{6,4},{7,5},{8,10},{9,11},{10,... | collective-permute-start | bytes 196616 | tf_op jit(solution)/shard_map/ppermute | solution.py:380
  59.0 8.7 %collective-permute-start.24 = (bf16[32,1152]{1,0:T(8,128)(2,1)S(1)}, bf16[32,1152]{1,0:T(8,128)(2,1)S(1)}, u32[]{:S(2)}, u32[]{:S(2)}) collective-permute-start(bf16[32,1152]{1,0:T(8,128)(2,1)S(1)} %get-tuple-element.55), channel_id=1, source_target_pairs={{0,8},{1,9},{2,10},{3,11},{4,12},{5,13},{6,14},{16,24},{17,25},{18... | collective-permute-start | bytes 221192 | tf_op jit(solution)/shard_map/ppermute | solution.py:380
  70.1 5.1 %collective-permute-start.26 = (bf16[32,1152]{1,0:T(8,128)(2,1)S(1)}, bf16[32,1152]{1,0:T(8,128)(2,1)S(1)}, u32[]{:S(2)}, u32[]{:S(2)}) collective-permute-start(bf16[32,1152]{1,0:T(8,128)(2,1)S(1)} %get-tuple-element.69), channel_id=1, source_target_pairs={{0,2},{1,3},{2,0},{3,1},{4,6},{5,7},{6,4},{7,5},{8,10},{9,11},{10,... | collective-permute-start | bytes 221192 | tf_op jit(solution)/shard_map/ppermute | solution.py:380
  70.6 5.6 %collective-permute-start.27 = (bf16[32,1152]{1,0:T(8,128)(2,1)S(1)}, bf16[32,1152]{1,0:T(8,128)(2,1)S(1)}, u32[]{:S(2)}, u32[]{:S(2)}) collective-permute-start(bf16[32,1152]{1,0:T(8,128)(2,1)S(1)} %get-tuple-element.70), channel_id=1, source_target_pairs={{0,3},{1,2},{2,1},{3,0},{4,7},{5,6},{6,5},{7,4},{8,11},{9,10},{10,... | collective-permute-start | bytes 221192 | tf_op jit(solution)/shard_map/ppermute | solution.py:380
  71.8 5.1 %collective-permute-start.28 = (bf16[32,1152]{1,0:T(8,128)(2,1)S(1)}, bf16[32,1152]{1,0:T(8,128)(2,1)S(1)}, u32[]{:S(2)}, u32[]{:S(2)}) collective-permute-start(bf16[32,1152]{1,0:T(8,128)(2,1)S(1)} %get-tuple-element.71), channel_id=1, source_target_pairs={{0,4},{1,5},{2,6},{3,7},{4,0},{5,1},{6,2},{7,3},{8,12},{9,13},{10,... | collective-permute-start | bytes 221192 | tf_op jit(solution)/shard_map/ppermute | solution.py:380
  72.2 5.3 %collective-permute-start.29 = (bf16[32,1152]{1,0:T(8,128)(2,1)S(1)}, bf16[32,1152]{1,0:T(8,128)(2,1)S(1)}, u32[]{:S(2)}, u32[]{:S(2)}) collective-permute-start(bf16[32,1152]{1,0:T(8,128)(2,1)S(1)} %get-tuple-element.72), channel_id=1, source_target_pairs={{0,5},{1,4},{2,7},{3,6},{4,1},{5,0},{6,3},{7,2},{8,13},{9,12},{10,... | collective-permute-start | bytes 221192 | tf_op jit(solution)/shard_map/ppermute | solution.py:380
  73.6 6.3 %collective-permute-start.30 = (bf16[32,1152]{1,0:T(8,128)(2,1)S(1)}, bf16[32,1152]{1,0:T(8,128)(2,1)S(1)}, u32[]{:S(2)}, u32[]{:S(2)}) collective-permute-start(bf16[32,1152]{1,0:T(8,128)(2,1)S(1)} %get-tuple-element.73), channel_id=1, source_target_pairs={{0,6},{1,7},{2,4},{3,5},{4,2},{5,3},{6,0},{7,1},{8,14},{9,15},{10,... | collective-permute-start | bytes 221192 | tf_op jit(solution)/shard_map/ppermute | solution.py:380
  75.3 5.5 %collective-permute-start.31 = (bf16[32,1152]{1,0:T(8,128)(2,1)S(1)}, bf16[32,1152]{1,0:T(8,128)(2,1)S(1)}, u32[]{:S(2)}, u32[]{:S(2)}) collective-permute-start(bf16[32,1152]{1,0:T(8,128)(2,1)S(1)} %get-tuple-element.74), channel_id=1, source_target_pairs={{0,7},{1,6},{2,5},{3,4},{4,3},{5,2},{6,1},{7,0},{8,15},{9,14},{10,... | collective-permute-start | bytes 221192 | tf_op jit(solution)/shard_map/ppermute | solution.py:380
  76.2 14.4 %collective-permute-start.32 = (bf16[128,1024]{1,0:T(8,128)(2,1)S(1)}, bf16[128,1024]{1,0:T(8,128)(2,1)S(1)}, u32[]{:S(2)}, u32[]{:S(2)}) collective-permute-start(bf16[128,1024]{1,0:T(8,128)(2,1)S(1)} %get-tuple-element.75.refs_8_), channel_id=1, source_target_pairs={{0,1},{1,0},{2,3},{3,2},{4,5},{5,4},{6,7},{7,6},{8,9},{9,8},{10,11... | collective-permute-start | bytes 786440 | tf_op jit(solution)/shard_map/ppermute | solution.py:380
  80.9 9.2 %collective-permute-start.33 = (f32[8,256]{1,0:T(8,128)S(1)}, f32[8,256]{1,0:T(8,128)S(1)}, u32[]{:S(2)}, u32[]{:S(2)}) collective-permute-start(f32[8,256]{1,0:T(8,128)S(1)} %shard_map.57), channel_id=1, source_target_pairs={{0,8},{1,9},{2,10},{3,11},{4,12},{5,13},{6,14},{7,15},{8,0},{9,1},... | collective-permute-start | bytes 24584 | tf_op jit(solution)/shard_map/ppermute | solution.py:380
  (12 other events, 40.9 us)
